TPU v7x, 256 devices: a whole 4x4x8 slice. The times are simulated.
256 devices in a mesh: pipe: 8 (over x_hi, y), dp: 32 (over z, x_lo, core).
Axes of the slice: x: 4 (x_hi: 2, x_lo: 2; x = x_hi * 2 + x_lo), y: 4, z: 8, core: 2. Of those that a mesh axis runs over, the one named last changes fastest.
Arguments:
- video: bfloat16 [4, 32, 3, 16, 8, 128], P(None, 'dp'), may hold values from -6 to 6
- cotangent: bfloat16 [4, 32, 3, 16, 8, 128], P(None, 'dp'), may hold values from -6 to 6
- weights: bfloat16 [8, 3456, 128], P('pipe'), may hold values from -0.109375 to 0.109375
- gains: float32 [8, 128], P('pipe'), may hold values from 0.1 to 1.9
Outputs:
- segment_out: bfloat16 [8, 4, 32, 3, 16, 8, 128], P('pipe', None, 'dp')
- in_grad: bfloat16 [8, 4, 32, 3, 16, 8, 128], P('pipe', None, 'dp')
- weight_grad: float32 [8, 442368], P('pipe', 'dp')
All inputs are finite; a program needn't handle non-finite values.
Results may differ from a plain program's by a relative error of at most 0.025.
Values may be sent and summed in bfloat16 or wider, within the bound.
A program may use at most 64 MiB of HBM per device.

v0:
```python
import math

import jax
import jax.numpy as jnp
from jax import lax
from jax.sharding import PartitionSpec as P

GROUPS = 32


def shifted(value, axis, steps):
    count = lax.axis_size(axis)
    initial, last = (max(0, -steps), min(count, count - steps))
    return lax.ppermute(value, axis, [(source, source + steps) for source in range(initial, last)])


def split_up(array, dim, devices):
    dims = array.shape
    pieces = array.reshape(*dims[:dim], devices, dims[dim] // devices, *dims[dim + 1 :])
    return jnp.moveaxis(pieces, dim, 0)


def sent_and_summed(array, axis, dim):
    pieces = split_up(array, dim, lax.axis_size(axis))
    arrived = lax.all_to_all(pieces, axis, split_axis=0, concat_axis=0, tiled=True)
    return arrived.astype(jnp.float32).sum(axis=0)


def norm_act(values, gain):
    batch, frames, rows, cols, chans = values.shape
    grouped = values.reshape(batch, frames, rows, cols, GROUPS, chans // GROUPS)
    mean = jnp.mean(grouped, axis=(1, 2, 3, 5), keepdims=True)
    centred = grouped - mean
    var = jnp.mean(centred * centred, axis=(1, 2, 3, 5), keepdims=True)
    normed = (centred * lax.rsqrt(var + 1e-06)).reshape(values.shape) * gain
    return jax.nn.silu(normed)


def patches(act):
    frames, rows, cols = (act.shape[1], act.shape[2], act.shape[3])
    leading = act[:, :1]
    padded = jnp.concatenate([leading, leading, act], axis=1)
    padded = jnp.pad(padded, ((0, 0), (0, 0), (1, 1), (1, 1), (0, 0)))
    pieces = [
        padded[
            :, frame_off : frame_off + frames, row_off : row_off + rows, col_off : col_off + cols, :
        ]
        for frame_off in range(3)
        for row_off in range(3)
        for col_off in range(3)
    ]
    return jnp.concatenate(pieces, axis=-1).reshape(-1, 27 * act.shape[-1])


def forward(inputs, weight, gain):
    values = inputs.astype(jnp.float32)
    act = norm_act(values, gain).astype(jnp.bfloat16)
    cols_mat = patches(act)
    branch = jnp.dot(cols_mat, weight, preferred_element_type=jnp.float32).reshape(inputs.shape)
    return ((values + branch).astype(jnp.bfloat16), cols_mat)


def backward(inputs, grad, weight, gain, cols_mat):
    values = inputs.astype(jnp.float32)
    flat_grad = grad.reshape(-1, grad.shape[-1])
    term = lax.dot_general(
        cols_mat, flat_grad, (((0,), (0,)), ((), ())), preferred_element_type=jnp.float32
    )
    grad_cols = lax.dot_general(
        flat_grad, weight, (((1,), (1,)), ((), ())), preferred_element_type=jnp.float32
    )
    _, pull_cols = jax.vjp(patches, jnp.zeros(inputs.shape, jnp.float32))
    grad_act = pull_cols(grad_cols)[0]
    _, pull_norm = jax.vjp(lambda field: norm_act(field, gain), values)
    grad_in = grad.astype(jnp.float32) + pull_norm(grad_act)[0]
    return (grad_in.astype(jnp.bfloat16), term)


def place(buffer, slot, value, valid):
    older = lax.dynamic_index_in_dim(buffer, slot, 0, False)
    return lax.dynamic_update_index_in_dim(buffer, jnp.where(valid, value, older), slot, 0)


def body(video, cotangent, weights, gains):
    segment = lax.axis_index("pipe")
    sections = lax.axis_size("pipe")
    micro = video.shape[0]
    ticks = micro + sections - 1
    weight = weights[0]
    gain = gains[0]
    is_first = segment == 0
    is_last = segment == sections - 1
    unit_shape = video.shape[1:]
    kept_init = jnp.zeros((1, 1), jnp.bfloat16)

    def forward_tick(carry, tick):
        received, saved, outputs, kept = carry
        index = tick - segment
        valid = (index >= 0) & (index < micro)
        slot = jnp.clip(index, 0, micro - 1)
        unit_in = jnp.where(is_first, lax.dynamic_index_in_dim(video, slot, 0, False), received)
        result, cols_mat = forward(unit_in, weight, gain)
        saved = place(saved, slot, unit_in, valid)
        outputs = place(outputs, slot, result, valid)
        received = shifted(result, "pipe", 1)
        return ((received, saved, outputs, kept), None)

    empty = jnp.zeros(video.shape, jnp.bfloat16)
    start = (jnp.zeros(unit_shape, jnp.bfloat16), empty, empty, kept_init)
    (_, saved, outputs, kept), _ = lax.scan(forward_tick, start, jnp.arange(ticks, dtype=jnp.int32))
    total_init = jnp.zeros(weight.shape, jnp.float32)

    def backward_tick(carry, tick):
        received, grads_out, total = carry
        index = tick - (sections - 1 - segment)
        valid = (index >= 0) & (index < micro)
        slot = jnp.clip(index, 0, micro - 1)
        grad = jnp.where(is_last, lax.dynamic_index_in_dim(cotangent, slot, 0, False), received)
        unit_in = lax.dynamic_index_in_dim(saved, slot, 0, False)
        cols_mat = patches(norm_act(unit_in.astype(jnp.float32), gain).astype(jnp.bfloat16))
        grad_in, term = backward(unit_in, grad, weight, gain, cols_mat)
        term = jnp.where(valid, term, 0.0)
        total = total + term
        grads_out = place(grads_out, slot, grad_in, valid)
        received = shifted(grad_in, "pipe", -1)
        return ((received, grads_out, total), None)

    start_back = (jnp.zeros(unit_shape, jnp.bfloat16), empty, total_init)
    (_, grads_out, total), _ = lax.scan(
        backward_tick, start_back, jnp.arange(ticks, dtype=jnp.int32)
    )
    share = sent_and_summed(total.reshape(-1).astype(jnp.bfloat16), "dp", 0)
    clip_total = unit_shape[0] * lax.axis_size("dp")
    scale = 1.0 / math.sqrt(micro * clip_total * unit_shape[1] * unit_shape[2] * unit_shape[3])
    return (outputs[None], grads_out[None], (share * scale)[None])


def solution(mesh):
    in_specs = (
        P(None, "dp", None, None, None, None),
        P(None, "dp", None, None, None, None),
        P("pipe", None, None),
        P("pipe", None),
    )
    out_specs = (
        P("pipe", None, "dp", None, None, None, None),
        P("pipe", None, "dp", None, None, None, None),
        P("pipe", "dp"),
    )
    return jax.shard_map(body, mesh=mesh, in_specs=in_specs, out_specs=out_specs, check_vma=False)
```

profile of v0, /device:TPU:6, one launch (start us, length us, event | category | flops | bytes accessed | tf_op | source)
XLA Modules:
  0.0 477.3 jit_solution(2412098222261372460)
XLA Ops:
  0.8 181.2 %while.33 = (s32[]{:T(128)}, bf16[1,3,16,8,128]{4,3,2,1,0:T(8,128)(2,1)S(1)}, bf16[4,1,3,16,8,128]{5,4,3,2,1,0:T(8,128)(2,1)S(1)}, bf16[4,1,3,16,8,128]{5,4,3,2,...) while((s32[]{:T(128)}, ...), condition=%wide.region_5.6_spmd, body=%wide.region_0.5_spmd.sunk | while | flops 341573664 | bytes 16430921 | solution.py:110
  10.7 6.6 %collective-permute-done = bf16[1,3,16,8,128]{4,3,2,1,0:T(8,128)(2,1)S(1)} collective-permute-done((bf16[1,3,16,8,128]{4,3,2,1,0:T(8,128)(2,1)S(1)}, bf16[1,3,16,8,128]{4,3,2,1,0:T(8,128)(2,1)S(1)}, u32[]{:S(2)}, u32[]{:S(2)}) %collective-permute-start) | collective-permute-done | bytes 98336 | tf_op jit(solution)/shard_map/while/body/eval_jaxpr/ppermute | solution.py:14
  25.6 8.2 %collective-permute-done = bf16[1,3,16,8,128]{4,3,2,1,0:T(8,128)(2,1)S(1)} collective-permute-done((bf16[1,3,16,8,128]{4,3,2,1,0:T(8,128)(2,1)S(1)}, bf16[1,3,16,8,128]{4,3,2,1,0:T(8,128)(2,1)S(1)}, u32[]{:S(2)}, u32[]{:S(2)}) %collective-permute-start) | collective-permute-done | bytes 98336 | tf_op jit(solution)/shard_map/while/body/eval_jaxpr/ppermute | solution.py:14
  42.1 8.2 %collective-permute-done = bf16[1,3,16,8,128]{4,3,2,1,0:T(8,128)(2,1)S(1)} collective-permute-done((bf16[1,3,16,8,128]{4,3,2,1,0:T(8,128)(2,1)S(1)}, bf16[1,3,16,8,128]{4,3,2,1,0:T(8,128)(2,1)S(1)}, u32[]{:S(2)}, u32[]{:S(2)}) %collective-permute-start) | collective-permute-done | bytes 98336 | tf_op jit(solution)/shard_map/while/body/eval_jaxpr/ppermute | solution.py:14
  58.5 8.2 %collective-permute-done = bf16[1,3,16,8,128]{4,3,2,1,0:T(8,128)(2,1)S(1)} collective-permute-done((bf16[1,3,16,8,128]{4,3,2,1,0:T(8,128)(2,1)S(1)}, bf16[1,3,16,8,128]{4,3,2,1,0:T(8,128)(2,1)S(1)}, u32[]{:S(2)}, u32[]{:S(2)}) %collective-permute-start) | collective-permute-done | bytes 98336 | tf_op jit(solution)/shard_map/while/body/eval_jaxpr/ppermute | solution.py:14
  75.0 8.2 %collective-permute-done = bf16[1,3,16,8,128]{4,3,2,1,0:T(8,128)(2,1)S(1)} collective-permute-done((bf16[1,3,16,8,128]{4,3,2,1,0:T(8,128)(2,1)S(1)}, bf16[1,3,16,8,128]{4,3,2,1,0:T(8,128)(2,1)S(1)}, u32[]{:S(2)}, u32[]{:S(2)}) %collective-permute-start) | collective-permute-done | bytes 98336 | tf_op jit(solution)/shard_map/while/body/eval_jaxpr/ppermute | solution.py:14
  91.5 8.2 %collective-permute-done = bf16[1,3,16,8,128]{4,3,2,1,0:T(8,128)(2,1)S(1)} collective-permute-done((bf16[1,3,16,8,128]{4,3,2,1,0:T(8,128)(2,1)S(1)}, bf16[1,3,16,8,128]{4,3,2,1,0:T(8,128)(2,1)S(1)}, u32[]{:S(2)}, u32[]{:S(2)}) %collective-permute-start) | collective-permute-done | bytes 98336 | tf_op jit(solution)/shard_map/while/body/eval_jaxpr/ppermute | solution.py:14
  107.9 8.2 %collective-permute-done = bf16[1,3,16,8,128]{4,3,2,1,0:T(8,128)(2,1)S(1)} collective-permute-done((bf16[1,3,16,8,128]{4,3,2,1,0:T(8,128)(2,1)S(1)}, bf16[1,3,16,8,128]{4,3,2,1,0:T(8,128)(2,1)S(1)}, u32[]{:S(2)}, u32[]{:S(2)}) %collective-permute-start) | collective-permute-done | bytes 98336 | tf_op jit(solution)/shard_map/while/body/eval_jaxpr/ppermute | solution.py:14
  124.4 8.2 %collective-permute-done = bf16[1,3,16,8,128]{4,3,2,1,0:T(8,128)(2,1)S(1)} collective-permute-done((bf16[1,3,16,8,128]{4,3,2,1,0:T(8,128)(2,1)S(1)}, bf16[1,3,16,8,128]{4,3,2,1,0:T(8,128)(2,1)S(1)}, u32[]{:S(2)}, u32[]{:S(2)}) %collective-permute-start) | collective-permute-done | bytes 98336 | tf_op jit(solution)/shard_map/while/body/eval_jaxpr/ppermute | solution.py:14
  140.9 8.2 %collective-permute-done = bf16[1,3,16,8,128]{4,3,2,1,0:T(8,128)(2,1)S(1)} collective-permute-done((bf16[1,3,16,8,128]{4,3,2,1,0:T(8,128)(2,1)S(1)}, bf16[1,3,16,8,128]{4,3,2,1,0:T(8,128)(2,1)S(1)}, u32[]{:S(2)}, u32[]{:S(2)}) %collective-permute-start) | collective-permute-done | bytes 98336 | tf_op jit(solution)/shard_map/while/body/eval_jaxpr/ppermute | solution.py:14
  157.3 8.2 %collective-permute-done = bf16[1,3,16,8,128]{4,3,2,1,0:T(8,128)(2,1)S(1)} collective-permute-done((bf16[1,3,16,8,128]{4,3,2,1,0:T(8,128)(2,1)S(1)}, bf16[1,3,16,8,128]{4,3,2,1,0:T(8,128)(2,1)S(1)}, u32[]{:S(2)}, u32[]{:S(2)}) %collective-permute-start) | collective-permute-done | bytes 98336 | tf_op jit(solution)/shard_map/while/body/eval_jaxpr/ppermute | solution.py:14
  173.8 8.2 %collective-permute-done = bf16[1,3,16,8,128]{4,3,2,1,0:T(8,128)(2,1)S(1)} collective-permute-done((bf16[1,3,16,8,128]{4,3,2,1,0:T(8,128)(2,1)S(1)}, bf16[1,3,16,8,128]{4,3,2,1,0:T(8,128)(2,1)S(1)}, u32[]{:S(2)}, u32[]{:S(2)}) %collective-permute-start) | collective-permute-done | bytes 98336 | tf_op jit(solution)/shard_map/while/body/eval_jaxpr/ppermute | solution.py:14
  182.9 247.0 %while.34 = (s32[]{:T(128)}, bf16[1,3,16,8,128]{4,3,2,1,0:T(8,128)(2,1)S(1)}, bf16[4,1,3,16,8,128]{5,4,3,2,1,0:T(8,128)(2,1)}, f32[3456,128]{1,0:T(8,128)}, pred...) while((s32[]{:T(128)}, ...), condition=%wide.region_15.16_spmd.clone, body=%wide.region_6.15_spmd.clone.sunk | while | flops 686339328 | bytes 53340172 | solution.py:129
  214.7 5.3 %collective-permute-start.1 = (bf16[1,3,16,8,128]{4,3,2,1,0:T(8,128)(2,1)S(1)}, bf16[1,3,16,8,128]{4,3,2,1,0:T(8,128)(2,1)S(1)}, u32[]{:S(2)}, u32[]{:S(2)}) collective-permute-start(bf16[1,3,16,8,128]{4,3,2,1,0:T(8,128)(2,1)S(1)} %get-tuple-element.587), channel_id=1, source_target_pairs={{32,0},{64,32},{96,64},{128,96},{160,128},{192,160},{224,192},{33,... | collective-permute-start | bytes 294920 | tf_op jit(solution)/shard_map/while/body/eval_jaxpr/ppermute | solution.py:14
  237.4 5.3 %collective-permute-start.1 = (bf16[1,3,16,8,128]{4,3,2,1,0:T(8,128)(2,1)S(1)}, bf16[1,3,16,8,128]{4,3,2,1,0:T(8,128)(2,1)S(1)}, u32[]{:S(2)}, u32[]{:S(2)}) collective-permute-start(bf16[1,3,16,8,128]{4,3,2,1,0:T(8,128)(2,1)S(1)} %get-tuple-element.587), channel_id=1, source_target_pairs={{32,0},{64,32},{96,64},{128,96},{160,128},{192,160},{224,192},{33,... | collective-permute-start | bytes 294920 | tf_op jit(solution)/shard_map/while/body/eval_jaxpr/ppermute | solution.py:14
  260.0 5.3 %collective-permute-start.1 = (bf16[1,3,16,8,128]{4,3,2,1,0:T(8,128)(2,1)S(1)}, bf16[1,3,16,8,128]{4,3,2,1,0:T(8,128)(2,1)S(1)}, u32[]{:S(2)}, u32[]{:S(2)}) collective-permute-start(bf16[1,3,16,8,128]{4,3,2,1,0:T(8,128)(2,1)S(1)} %get-tuple-element.587), channel_id=1, source_target_pairs={{32,0},{64,32},{96,64},{128,96},{160,128},{192,160},{224,192},{33,... | collective-permute-start | bytes 294920 | tf_op jit(solution)/shard_map/while/body/eval_jaxpr/ppermute | solution.py:14
  282.7 5.3 %collective-permute-start.1 = (bf16[1,3,16,8,128]{4,3,2,1,0:T(8,128)(2,1)S(1)}, bf16[1,3,16,8,128]{4,3,2,1,0:T(8,128)(2,1)S(1)}, u32[]{:S(2)}, u32[]{:S(2)}) collective-permute-start(bf16[1,3,16,8,128]{4,3,2,1,0:T(8,128)(2,1)S(1)} %get-tuple-element.587), channel_id=1, source_target_pairs={{32,0},{64,32},{96,64},{128,96},{160,128},{192,160},{224,192},{33,... | collective-permute-start | bytes 294920 | tf_op jit(solution)/shard_map/while/body/eval_jaxpr/ppermute | solution.py:14
  305.4 5.3 %collective-permute-start.1 = (bf16[1,3,16,8,128]{4,3,2,1,0:T(8,128)(2,1)S(1)}, bf16[1,3,16,8,128]{4,3,2,1,0:T(8,128)(2,1)S(1)}, u32[]{:S(2)}, u32[]{:S(2)}) collective-permute-start(bf16[1,3,16,8,128]{4,3,2,1,0:T(8,128)(2,1)S(1)} %get-tuple-element.587), channel_id=1, source_target_pairs={{32,0},{64,32},{96,64},{128,96},{160,128},{192,160},{224,192},{33,... | collective-permute-start | bytes 294920 | tf_op jit(solution)/shard_map/while/body/eval_jaxpr/ppermute | solution.py:14
  350.7 5.3 %collective-permute-start.1 = (bf16[1,3,16,8,128]{4,3,2,1,0:T(8,128)(2,1)S(1)}, bf16[1,3,16,8,128]{4,3,2,1,0:T(8,128)(2,1)S(1)}, u32[]{:S(2)}, u32[]{:S(2)}) collective-permute-start(bf16[1,3,16,8,128]{4,3,2,1,0:T(8,128)(2,1)S(1)} %get-tuple-element.587), channel_id=1, source_target_pairs={{32,0},{64,32},{96,64},{128,96},{160,128},{192,160},{224,192},{33,... | collective-permute-start | bytes 294920 | tf_op jit(solution)/shard_map/while/body/eval_jaxpr/ppermute | solution.py:14
  373.3 6.3 %collective-permute-start.1 = (bf16[1,3,16,8,128]{4,3,2,1,0:T(8,128)(2,1)S(1)}, bf16[1,3,16,8,128]{4,3,2,1,0:T(8,128)(2,1)S(1)}, u32[]{:S(2)}, u32[]{:S(2)}) collective-permute-start(bf16[1,3,16,8,128]{4,3,2,1,0:T(8,128)(2,1)S(1)} %get-tuple-element.587), channel_id=1, source_target_pairs={{32,0},{64,32},{96,64},{128,96},{160,128},{192,160},{224,192},{33,... | collective-permute-start | bytes 294920 | tf_op jit(solution)/shard_map/while/body/eval_jaxpr/ppermute | solution.py:14
  397.0 5.5 %collective-permute-start.1 = (bf16[1,3,16,8,128]{4,3,2,1,0:T(8,128)(2,1)S(1)}, bf16[1,3,16,8,128]{4,3,2,1,0:T(8,128)(2,1)S(1)}, u32[]{:S(2)}, u32[]{:S(2)}) collective-permute-start(bf16[1,3,16,8,128]{4,3,2,1,0:T(8,128)(2,1)S(1)} %get-tuple-element.587), channel_id=1, source_target_pairs={{32,0},{64,32},{96,64},{128,96},{160,128},{192,160},{224,192},{33,... | collective-permute-start | bytes 294920 | tf_op jit(solution)/shard_map/while/body/eval_jaxpr/ppermute | solution.py:14
  419.8 5.3 %collective-permute-start.1 = (bf16[1,3,16,8,128]{4,3,2,1,0:T(8,128)(2,1)S(1)}, bf16[1,3,16,8,128]{4,3,2,1,0:T(8,128)(2,1)S(1)}, u32[]{:S(2)}, u32[]{:S(2)}) collective-permute-start(bf16[1,3,16,8,128]{4,3,2,1,0:T(8,128)(2,1)S(1)} %get-tuple-element.587), channel_id=1, source_target_pairs={{32,0},{64,32},{96,64},{128,96},{160,128},{192,160},{224,192},{33,... | collective-permute-start | bytes 294920 | tf_op jit(solution)/shard_map/while/body/eval_jaxpr/ppermute | solution.py:14
  432.6 6.0 %reduce.60 = bf16[32,13824]{1,0:T(8,128)(2,1)S(1)} reduce(bf16[32,1,13824]{2,1,0:T(2,128)(2,1)S(1)} %convert_element_type.151, bf16[]{:T(256)} %broadcast.501), dimensions={1}, to_apply=%convert_element_type.151.reduce_sub_computation | reduce | bytes 1769474 | tf_op jit(solution)/shard_map/convert_element_type | solution.py:132
  438.8 35.3 %all_to_all.6 = bf16[32,2,6912]{2,1,0:T(2,128)(2,1)S(1)} all-to-all(bf16[32,2,6912]{2,1,0:T(2,128)(2,1)S(1)} %reshape.390), channel_id=1, replica_groups=mesh['pipe'=8,'dp'=32] {'dp'}, dimensions={0} | all-to-all | bytes 1769472 | tf_op jit(solution)/shard_map/all_to_all | solution.py:25
  (1351 shorter events, 277.8 us)
Async XLA Ops:
  7.2 10.1 %collective-permute-start = (bf16[1,3,16,8,128]{4,3,2,1,0:T(8,128)(2,1)S(1)}, bf16[1,3,16,8,128]{4,3,2,1,0:T(8,128)(2,1)S(1)}, u32[]{:S(2)}, u32[]{:S(2)}) collective-permute-start(bf16[1,3,16,8,128]{4,3,2,1,0:T(8,128)(2,1)S(1)} %get-tuple-element.544), channel_id=1, source_target_pairs={{0,32},{32,64},{64,96},{96,128},{128,160},{160,192},{192,224},{1,3... | collective-permute-start | bytes 294920 | tf_op jit(solution)/shard_map/while/body/eval_jaxpr/ppermute | solution.py:14
  23.7 10.1 %collective-permute-start = (bf16[1,3,16,8,128]{4,3,2,1,0:T(8,128)(2,1)S(1)}, bf16[1,3,16,8,128]{4,3,2,1,0:T(8,128)(2,1)S(1)}, u32[]{:S(2)}, u32[]{:S(2)}) collective-permute-start(bf16[1,3,16,8,128]{4,3,2,1,0:T(8,128)(2,1)S(1)} %get-tuple-element.544), channel_id=1, source_target_pairs={{0,32},{32,64},{64,96},{96,128},{128,160},{160,192},{192,224},{1,3... | collective-permute-start | bytes 294920 | tf_op jit(solution)/shard_map/while/body/eval_jaxpr/ppermute | solution.py:14
  40.1 10.1 %collective-permute-start = (bf16[1,3,16,8,128]{4,3,2,1,0:T(8,128)(2,1)S(1)}, bf16[1,3,16,8,128]{4,3,2,1,0:T(8,128)(2,1)S(1)}, u32[]{:S(2)}, u32[]{:S(2)}) collective-permute-start(bf16[1,3,16,8,128]{4,3,2,1,0:T(8,128)(2,1)S(1)} %get-tuple-element.544), channel_id=1, source_target_pairs={{0,32},{32,64},{64,96},{96,128},{128,160},{160,192},{192,224},{1,3... | collective-permute-start | bytes 294920 | tf_op jit(solution)/shard_map/while/body/eval_jaxpr/ppermute | solution.py:14
  56.6 10.1 %collective-permute-start = (bf16[1,3,16,8,128]{4,3,2,1,0:T(8,128)(2,1)S(1)}, bf16[1,3,16,8,128]{4,3,2,1,0:T(8,128)(2,1)S(1)}, u32[]{:S(2)}, u32[]{:S(2)}) collective-permute-start(bf16[1,3,16,8,128]{4,3,2,1,0:T(8,128)(2,1)S(1)} %get-tuple-element.544), channel_id=1, source_target_pairs={{0,32},{32,64},{64,96},{96,128},{128,160},{160,192},{192,224},{1,3... | collective-permute-start | bytes 294920 | tf_op jit(solution)/shard_map/while/body/eval_jaxpr/ppermute | solution.py:14
  73.1 10.1 %collective-permute-start = (bf16[1,3,16,8,128]{4,3,2,1,0:T(8,128)(2,1)S(1)}, bf16[1,3,16,8,128]{4,3,2,1,0:T(8,128)(2,1)S(1)}, u32[]{:S(2)}, u32[]{:S(2)}) collective-permute-start(bf16[1,3,16,8,128]{4,3,2,1,0:T(8,128)(2,1)S(1)} %get-tuple-element.544), channel_id=1, source_target_pairs={{0,32},{32,64},{64,96},{96,128},{128,160},{160,192},{192,224},{1,3... | collective-permute-start | bytes 294920 | tf_op jit(solution)/shard_map/while/body/eval_jaxpr/ppermute | solution.py:14
  89.5 10.1 %collective-permute-start = (bf16[1,3,16,8,128]{4,3,2,1,0:T(8,128)(2,1)S(1)}, bf16[1,3,16,8,128]{4,3,2,1,0:T(8,128)(2,1)S(1)}, u32[]{:S(2)}, u32[]{:S(2)}) collective-permute-start(bf16[1,3,16,8,128]{4,3,2,1,0:T(8,128)(2,1)S(1)} %get-tuple-element.544), channel_id=1, source_target_pairs={{0,32},{32,64},{64,96},{96,128},{128,160},{160,192},{192,224},{1,3... | collective-permute-start | bytes 294920 | tf_op jit(solution)/shard_map/while/body/eval_jaxpr/ppermute | solution.py:14
  106.0 10.1 %collective-permute-start = (bf16[1,3,16,8,128]{4,3,2,1,0:T(8,128)(2,1)S(1)}, bf16[1,3,16,8,128]{4,3,2,1,0:T(8,128)(2,1)S(1)}, u32[]{:S(2)}, u32[]{:S(2)}) collective-permute-start(bf16[1,3,16,8,128]{4,3,2,1,0:T(8,128)(2,1)S(1)} %get-tuple-element.544), channel_id=1, source_target_pairs={{0,32},{32,64},{64,96},{96,128},{128,160},{160,192},{192,224},{1,3... | collective-permute-start | bytes 294920 | tf_op jit(solution)/shard_map/while/body/eval_jaxpr/ppermute | solution.py:14
  122.5 10.1 %collective-permute-start = (bf16[1,3,16,8,128]{4,3,2,1,0:T(8,128)(2,1)S(1)}, bf16[1,3,16,8,128]{4,3,2,1,0:T(8,128)(2,1)S(1)}, u32[]{:S(2)}, u32[]{:S(2)}) collective-permute-start(bf16[1,3,16,8,128]{4,3,2,1,0:T(8,128)(2,1)S(1)} %get-tuple-element.544), channel_id=1, source_target_pairs={{0,32},{32,64},{64,96},{96,128},{128,160},{160,192},{192,224},{1,3... | collective-permute-start | bytes 294920 | tf_op jit(solution)/shard_map/while/body/eval_jaxpr/ppermute | solution.py:14
  138.9 10.1 %collective-permute-start = (bf16[1,3,16,8,128]{4,3,2,1,0:T(8,128)(2,1)S(1)}, bf16[1,3,16,8,128]{4,3,2,1,0:T(8,128)(2,1)S(1)}, u32[]{:S(2)}, u32[]{:S(2)}) collective-permute-start(bf16[1,3,16,8,128]{4,3,2,1,0:T(8,128)(2,1)S(1)} %get-tuple-element.544), channel_id=1, source_target_pairs={{0,32},{32,64},{64,96},{96,128},{128,160},{160,192},{192,224},{1,3... | collective-permute-start | bytes 294920 | tf_op jit(solution)/shard_map/while/body/eval_jaxpr/ppermute | solution.py:14
  155.4 10.1 %collective-permute-start = (bf16[1,3,16,8,128]{4,3,2,1,0:T(8,128)(2,1)S(1)}, bf16[1,3,16,8,128]{4,3,2,1,0:T(8,128)(2,1)S(1)}, u32[]{:S(2)}, u32[]{:S(2)}) collective-permute-start(bf16[1,3,16,8,128]{4,3,2,1,0:T(8,128)(2,1)S(1)} %get-tuple-element.544), channel_id=1, source_target_pairs={{0,32},{32,64},{64,96},{96,128},{128,160},{160,192},{192,224},{1,3... | collective-permute-start | bytes 294920 | tf_op jit(solution)/shard_map/while/body/eval_jaxpr/ppermute | solution.py:14
  171.9 10.1 %collective-permute-start = (bf16[1,3,16,8,128]{4,3,2,1,0:T(8,128)(2,1)S(1)}, bf16[1,3,16,8,128]{4,3,2,1,0:T(8,128)(2,1)S(1)}, u32[]{:S(2)}, u32[]{:S(2)}) collective-permute-start(bf16[1,3,16,8,128]{4,3,2,1,0:T(8,128)(2,1)S(1)} %get-tuple-element.544), channel_id=1, source_target_pairs={{0,32},{32,64},{64,96},{96,128},{128,160},{160,192},{192,224},{1,3... | collective-permute-start | bytes 294920 | tf_op jit(solution)/shard_map/while/body/eval_jaxpr/ppermute | solution.py:14
  195.5 6.5 %collective-permute-start.1 = (bf16[1,3,16,8,128]{4,3,2,1,0:T(8,128)(2,1)S(1)}, bf16[1,3,16,8,128]{4,3,2,1,0:T(8,128)(2,1)S(1)}, u32[]{:S(2)}, u32[]{:S(2)}) collective-permute-start(bf16[1,3,16,8,128]{4,3,2,1,0:T(8,128)(2,1)S(1)} %get-tuple-element.587), channel_id=1, source_target_pairs={{32,0},{64,32},{96,64},{128,96},{160,128},{192,160},{224,192},{33,... | collective-permute-start | bytes 294920 | tf_op jit(solution)/shard_map/while/body/eval_jaxpr/ppermute | solution.py:14
  214.7 8.9 %collective-permute-start.1 = (bf16[1,3,16,8,128]{4,3,2,1,0:T(8,128)(2,1)S(1)}, bf16[1,3,16,8,128]{4,3,2,1,0:T(8,128)(2,1)S(1)}, u32[]{:S(2)}, u32[]{:S(2)}) collective-permute-start(bf16[1,3,16,8,128]{4,3,2,1,0:T(8,128)(2,1)S(1)} %get-tuple-element.587), channel_id=1, source_target_pairs={{32,0},{64,32},{96,64},{128,96},{160,128},{192,160},{224,192},{33,... | collective-permute-start | bytes 294920 | tf_op jit(solution)/shard_map/while/body/eval_jaxpr/ppermute | solution.py:14
  230.9 3.7 copy-start.5
  237.4 8.9 %collective-permute-start.1 = (bf16[1,3,16,8,128]{4,3,2,1,0:T(8,128)(2,1)S(1)}, bf16[1,3,16,8,128]{4,3,2,1,0:T(8,128)(2,1)S(1)}, u32[]{:S(2)}, u32[]{:S(2)}) collective-permute-start(bf16[1,3,16,8,128]{4,3,2,1,0:T(8,128)(2,1)S(1)} %get-tuple-element.587), channel_id=1, source_target_pairs={{32,0},{64,32},{96,64},{128,96},{160,128},{192,160},{224,192},{33,... | collective-permute-start | bytes 294920 | tf_op jit(solution)/shard_map/while/body/eval_jaxpr/ppermute | solution.py:14
  260.0 8.9 %collective-permute-start.1 = (bf16[1,3,16,8,128]{4,3,2,1,0:T(8,128)(2,1)S(1)}, bf16[1,3,16,8,128]{4,3,2,1,0:T(8,128)(2,1)S(1)}, u32[]{:S(2)}, u32[]{:S(2)}) collective-permute-start(bf16[1,3,16,8,128]{4,3,2,1,0:T(8,128)(2,1)S(1)} %get-tuple-element.587), channel_id=1, source_target_pairs={{32,0},{64,32},{96,64},{128,96},{160,128},{192,160},{224,192},{33,... | collective-permute-start | bytes 294920 | tf_op jit(solution)/shard_map/while/body/eval_jaxpr/ppermute | solution.py:14
  276.2 3.7 copy-start.5
  282.7 8.9 %collective-permute-start.1 = (bf16[1,3,16,8,128]{4,3,2,1,0:T(8,128)(2,1)S(1)}, bf16[1,3,16,8,128]{4,3,2,1,0:T(8,128)(2,1)S(1)}, u32[]{:S(2)}, u32[]{:S(2)}) collective-permute-start(bf16[1,3,16,8,128]{4,3,2,1,0:T(8,128)(2,1)S(1)} %get-tuple-element.587), channel_id=1, source_target_pairs={{32,0},{64,32},{96,64},{128,96},{160,128},{192,160},{224,192},{33,... | collective-permute-start | bytes 294920 | tf_op jit(solution)/shard_map/while/body/eval_jaxpr/ppermute | solution.py:14
  305.4 8.9 %collective-permute-start.1 = (bf16[1,3,16,8,128]{4,3,2,1,0:T(8,128)(2,1)S(1)}, bf16[1,3,16,8,128]{4,3,2,1,0:T(8,128)(2,1)S(1)}, u32[]{:S(2)}, u32[]{:S(2)}) collective-permute-start(bf16[1,3,16,8,128]{4,3,2,1,0:T(8,128)(2,1)S(1)} %get-tuple-element.587), channel_id=1, source_target_pairs={{32,0},{64,32},{96,64},{128,96},{160,128},{192,160},{224,192},{33,... | collective-permute-start | bytes 294920 | tf_op jit(solution)/shard_map/while/body/eval_jaxpr/ppermute | solution.py:14
  328.0 8.9 %collective-permute-start.1 = (bf16[1,3,16,8,128]{4,3,2,1,0:T(8,128)(2,1)S(1)}, bf16[1,3,16,8,128]{4,3,2,1,0:T(8,128)(2,1)S(1)}, u32[]{:S(2)}, u32[]{:S(2)}) collective-permute-start(bf16[1,3,16,8,128]{4,3,2,1,0:T(8,128)(2,1)S(1)} %get-tuple-element.587), channel_id=1, source_target_pairs={{32,0},{64,32},{96,64},{128,96},{160,128},{192,160},{224,192},{33,... | collective-permute-start | bytes 294920 | tf_op jit(solution)/shard_map/while/body/eval_jaxpr/ppermute | solution.py:14
  350.7 8.9 %collective-permute-start.1 = (bf16[1,3,16,8,128]{4,3,2,1,0:T(8,128)(2,1)S(1)}, bf16[1,3,16,8,128]{4,3,2,1,0:T(8,128)(2,1)S(1)}, u32[]{:S(2)}, u32[]{:S(2)}) collective-permute-start(bf16[1,3,16,8,128]{4,3,2,1,0:T(8,128)(2,1)S(1)} %get-tuple-element.587), channel_id=1, source_target_pairs={{32,0},{64,32},{96,64},{128,96},{160,128},{192,160},{224,192},{33,... | collective-permute-start | bytes 294920 | tf_op jit(solution)/shard_map/while/body/eval_jaxpr/ppermute | solution.py:14
  373.3 9.9 %collective-permute-start.1 = (bf16[1,3,16,8,128]{4,3,2,1,0:T(8,128)(2,1)S(1)}, bf16[1,3,16,8,128]{4,3,2,1,0:T(8,128)(2,1)S(1)}, u32[]{:S(2)}, u32[]{:S(2)}) collective-permute-start(bf16[1,3,16,8,128]{4,3,2,1,0:T(8,128)(2,1)S(1)} %get-tuple-element.587), channel_id=1, source_target_pairs={{32,0},{64,32},{96,64},{128,96},{160,128},{192,160},{224,192},{33,... | collective-permute-start | bytes 294920 | tf_op jit(solution)/shard_map/while/body/eval_jaxpr/ppermute | solution.py:14
  397.0 9.1 %collective-permute-start.1 = (bf16[1,3,16,8,128]{4,3,2,1,0:T(8,128)(2,1)S(1)}, bf16[1,3,16,8,128]{4,3,2,1,0:T(8,128)(2,1)S(1)}, u32[]{:S(2)}, u32[]{:S(2)}) collective-permute-start(bf16[1,3,16,8,128]{4,3,2,1,0:T(8,128)(2,1)S(1)} %get-tuple-element.587), channel_id=1, source_target_pairs={{32,0},{64,32},{96,64},{128,96},{160,128},{192,160},{224,192},{33,... | collective-permute-start | bytes 294920 | tf_op jit(solution)/shard_map/while/body/eval_jaxpr/ppermute | solution.py:14
  419.8 8.9 %collective-permute-start.1 = (bf16[1,3,16,8,128]{4,3,2,1,0:T(8,128)(2,1)S(1)}, bf16[1,3,16,8,128]{4,3,2,1,0:T(8,128)(2,1)S(1)}, u32[]{:S(2)}, u32[]{:S(2)}) collective-permute-start(bf16[1,3,16,8,128]{4,3,2,1,0:T(8,128)(2,1)S(1)} %get-tuple-element.587), channel_id=1, source_target_pairs={{32,0},{64,32},{96,64},{128,96},{160,128},{192,160},{224,192},{33,... | collective-permute-start | bytes 294920 | tf_op jit(solution)/shard_map/while/body/eval_jaxpr/ppermute | solution.py:14
  (54 other events, 87.6 us)
where the time goes:
time: 481 us; the launch traced here: 477 us
  local copies, waits for them, and re-layouts  109 us (23%)
  other arithmetic  91.7 us (19%)
  waiting for transfers between devices  89.6 us (19%)
  starting transfers between devices  78.9 us (16%)
  matrix products  52 us (11%)
  blocking collectives  35.3 us (7%)
  loops' own time  19.9 us (4%)
    ppermute x22, waiting for transfers between devices, shifted(): lax.ppermute(value, axis, [(source, source + steps) for source in range(i...  89.6 us
    ppermute x22, starting transfers between devices, shifted(): lax.ppermute(value, axis, [(source, source + steps) for source in range(i...  78.9 us
    while x649, local copies, waits for them, and re-layouts  42 us
    all_to_all x1, blocking collectives, sent_and_summed(): lax.all_to_all(pieces, axis, split_axis=0, concat_axis=0, tiled=True)  35.3 us
    add_any x11, other arithmetic, patches(): padded[:, frame_off:frame_off + frames, row_off:row_off + rows, col_off:c...  29.5 us
    dot_general x11, matrix products, backward(): lax.dot_general(flat_grad, weight, (((1,), (1,)), ((), ())), preferred_el...  22.5 us
    split x22, local copies, waits for them, and re-layouts, patches(): return jnp.concatenate(pieces, axis=-1).reshape(-1, 27 * act.shape[-1])  20.4 us
    dot_general x11, matrix products, backward(): lax.dot_general(cols_mat, flat_grad, (((0,), (0,)), ((), ())), preferred_...  19.8 us
  transfers between devices with their start and end apart: 22, of which 12 were waited for; matrix products, arithmetic and copies ran while one was open for 7% of the time, Pallas kernels for 0%

commit v1 on v0

v1 whole, which is shorter than its diff:
```python
import functools
import math

import jax
import jax.numpy as jnp
from jax import lax
from jax.experimental import pallas as pl
from jax.experimental.pallas import tpu as pltpu
from jax.sharding import PartitionSpec as P

GROUPS = 32
UNITS = 4
FRAMES, ROWS, COLS, C = 3, 16, 8, 128
PLANE = ROWS * COLS
PIX = FRAMES * PLANE
TAPS = 9
SLAB = TAPS * C
WROWS = 3 * SLAB
QUARTER = WROWS // 4
MESH = pl.DeviceIdType.MESH
F32, BF16 = jnp.float32, jnp.bfloat16


def group_sum(part):
    lane = lax.broadcasted_iota(jnp.int32, part.shape, 1)
    pair = part + jnp.where(lane % 2 == 0, pltpu.roll(part, C - 1, 1), pltpu.roll(part, 1, 1))
    quad = pair + jnp.where(lane % 4 < 2, pltpu.roll(pair, C - 2, 1), pltpu.roll(pair, 2, 1))
    return jnp.sum(quad, axis=0, keepdims=True)


def fill_shifts(field, dest, flip):
    col = lax.broadcasted_iota(jnp.int32, field.shape, 1)
    for col_off in range(3):
        step = (1 - col_off) if flip else (col_off - 1)
        if step == 0:
            moved = field
        elif step == 1:
            moved = jnp.where(col < COLS - 1, pltpu.roll(field, COLS - 1, 1), 0.0)
        else:
            moved = jnp.where(col > 0, pltpu.roll(field, 1, 1), 0.0)
        planes = moved.reshape(FRAMES, ROWS, COLS, C)
        blank = jnp.zeros((FRAMES, 1, COLS, C), F32)
        for row_off in range(3):
            step = (1 - row_off) if flip else (row_off - 1)
            if step == 0:
                rows = planes
            elif step == 1:
                rows = jnp.concatenate([planes[:, 1:], blank], axis=1)
            else:
                rows = jnp.concatenate([blank, planes[:, : ROWS - 1]], axis=1)
            at = (row_off * 3 + col_off) * C
            dest[:, at : at + C] = rows.reshape(PIX, C).astype(BF16)


def dot(lhs, rhs):
    return jnp.dot(lhs, rhs, preferred_element_type=F32)


def kernel(
    depth,
    scale,
    video,
    cot,
    w,
    gains,
    seg_out,
    grad_out,
    wg_out,
    wb,
    gbuf,
    xs,
    gs,
    acts,
    xhat_s,
    slope_s,
    rstd_s,
    shifts,
    actb,
    grdb,
    total,
    buf1,
    got1,
    buf2,
    got2,
    buf3,
    got3,
    load_sem,
    w_send,
    w_recv,
    gain_send,
    gain_recv,
    hop_send,
    hop_recv,
    out_send,
    seg_recv,
    act_recv,
    grd_recv,
    ing_recv,
    rs_send,
    rs_recv,
    z_send,
    z_recv,
):
    pipe = lax.axis_index("pipe")
    dp = lax.axis_index("dp")
    half = lax.div(pipe, UNITS)
    y = lax.rem(pipe, UNITS)
    core = lax.rem(dp, 2)
    x_lo = lax.rem(lax.div(dp, 2), 2)
    z = lax.div(dp, 4)
    base = half * UNITS
    yr = lax.rem(y + 1, UNITS)
    yo = lax.rem(y + 2, UNITS)
    yl = lax.rem(y + 3, UNITS)
    other_core = dp + 1 - 2 * core
    other_x = dp + 2 - 4 * x_lo
    other_half = pipe + UNITS - 2 * base

    def dev(pipe_at, dp_at):
        return (pipe_at, dp_at)

    def z_peer(step):
        return lax.rem(z + step, depth) * 4 + lax.rem(dp, 4)

    def remote(src, dst, send, recv, target):
        return pltpu.make_async_remote_copy(
            src_ref=src, dst_ref=dst, send_sem=send, recv_sem=recv, device_id=target, device_id_type=MESH
        )

    load_w = pltpu.make_async_copy(w, wb.at[y], load_sem.at[0])
    load_w.start()
    load_gain = pltpu.make_async_copy(gains, gbuf.at[y], load_sem.at[1])
    load_gain.start()

    @pl.when(half == 0)
    def _():
        pltpu.make_async_copy(video.at[y], xs.at[0], load_sem.at[2]).start()

    @pl.when(half == 1)
    def _():
        pltpu.make_async_copy(cot.at[y], gs.at[UNITS], load_sem.at[2]).start()

    barrier = pltpu.get_barrier_semaphore()
    peers = [dev(base + at, dp) for at in (yr, yo, yl)]
    peers += [dev(other_half, dp), dev(pipe, other_core), dev(pipe, other_x)]
    peers += [dev(pipe, z_peer(step)) for step in range(1, depth)]
    for peer in peers:
        pl.semaphore_signal(barrier, inc=1, device_id=peer, device_id_type=MESH)
    pl.semaphore_wait(barrier, len(peers))

    def gain_copy(at, slot):
        return remote(gains, gbuf.at[y], gain_send.at[slot], gain_recv.at[y], dev(base + at, dp))

    for slot, at in enumerate((yr, yo, yl)):
        gain_copy(at, slot).start()

    qa = core * 2
    qb = core * 2 + 1
    right, left, twin = dev(base + yr, dp), dev(base + yl, dp), dev(pipe, other_core)

    def rows_of(quarter):
        return pl.ds(pl.multiple_of(quarter * QUARTER, QUARTER), QUARTER)

    def own(quarter, slot, target):
        return remote(
            w.at[rows_of(quarter)],
            wb.at[y, rows_of(quarter)],
            w_send.at[slot],
            w_recv.at[y, quarter],
            target,
        )

    def relay(slab, quarter, slot, target):
        piece = wb.at[slab, rows_of(quarter)]
        return remote(piece, piece, w_send.at[slot], w_recv.at[slab, quarter], target)

    first = [own(qa, 0, right), own(qb, 1, left), own(qb, 2, right), own(qa, 3, left)]
    for copy in first:
        copy.start()
    relays = [
        (yl, qa, ((4, right), (6, twin))),
        (yr, qb, ((5, left), (7, twin))),
        (yl, qb, ((8, twin),)),
        (yr, qa, ((9, twin),)),
        (yo, qa, ((10, twin),)),
        (yo, qb, ((11, twin),)),
    ]
    sent = list(first)
    for slab, quarter, targets in relays:
        relay(slab, quarter, 0, right).wait_recv()
        for slot, target in targets:
            copy = relay(slab, quarter, slot, target)
            copy.start()
            sent.append(copy)
    qc = (1 - core) * 2
    for slab in (yl, yr, yo):
        for quarter in (qc, qc + 1):
            relay(slab, quarter, 0, twin).wait_recv()
    load_w.wait()
    load_gain.wait()
    for slot, at in enumerate((yr, yo, yl)):
        remote(gains, gbuf.at[at], gain_send.at[slot], gain_recv.at[at], dev(base + at, dp)).wait_recv()

    def to_home(src, dst, slot, recv, unit):
        away = remote(src, dst.at[y], out_send.at[slot, unit], recv.at[y], dev(base + unit, dp))
        here = pltpu.make_async_copy(src, dst.at[y], out_send.at[slot, unit])
        return away, here

    def start_home(*args):
        away, here = to_home(*args)
        unit = args[-1]

        @pl.when(unit != y)
        def _():
            away.start()

        @pl.when(unit == y)
        def _():
            here.start()

    def finish_home(*args):
        away, here = to_home(*args)
        unit = args[-1]

        @pl.when(unit != y)
        def _():
            away.wait_send()

        @pl.when(unit == y)
        def _():
            here.wait()

    def arrived(dst, recv):
        for at in (yr, yo, yl):
            remote(dst.at[at], dst.at[at], out_send.at[0, 0], recv.at[at], dev(base + at, dp)).wait_recv()

    hop_x = remote(xs.at[UNITS], xs.at[0], hop_send.at[0], hop_recv.at[0], dev(other_half, dp))
    hop_g = remote(gs.at[0], gs.at[UNITS], hop_send.at[1], hop_recv.at[1], dev(other_half, dp))

    @pl.when(half == 0)
    def _():
        pltpu.make_async_copy(video.at[y], xs.at[0], load_sem.at[2]).wait()

    @pl.when(half == 1)
    def _():
        pltpu.make_async_copy(cot.at[y], gs.at[UNITS], load_sem.at[2]).wait()
        hop_x.wait_recv()

    count = 1.0 / (PIX * (C // GROUPS))

    def forward(unit, _):
        gain = gbuf[unit].reshape(1, 1, C)
        x = xs[unit].astype(F32).reshape(PIX // COLS, COLS, C)
        mean = group_sum(jnp.sum(x, axis=0)) * count
        centred = x - mean.reshape(1, 1, C)
        var = group_sum(jnp.sum(centred * centred, axis=0)) * count
        rstd = lax.rsqrt(var + 1e-06)
        xhat = centred * rstd.reshape(1, 1, C)
        normed = xhat * gain
        sig = jax.nn.sigmoid(normed)
        act = normed * sig
        acts[unit] = act.reshape(PIX, C).astype(BF16)
        fill_shifts(act, shifts, False)
        xhat_s[unit] = xhat
        slope_s[unit] = (sig + act * (1.0 - sig)) * gain
        rstd_s[unit] = rstd
        part0 = dot(shifts[:PLANE], wb[unit, :SLAB])
        part1 = dot(shifts[: 2 * PLANE], wb[unit, SLAB : 2 * SLAB])
        part2 = dot(shifts[...], wb[unit, 2 * SLAB :])
        x = x.reshape(PIX, C)
        early = part0 + part1[:PLANE]
        branch = (early, early, part0 + part1[PLANE:])
        for frame in range(FRAMES):
            at = slice(frame * PLANE, (frame + 1) * PLANE)
            xs[unit + 1, at] = (x[at] + branch[frame] + part2[at]).astype(BF16)
        start_home(xs.at[unit + 1], seg_out, 0, seg_recv, unit)
        start_home(acts.at[unit], actb, 1, act_recv, unit)
        return 0

    lax.fori_loop(0, UNITS, forward, 0)

    @pl.when(half == 0)
    def _():
        hop_x.start()
        hop_g.wait_recv()

    def backward(step, _):
        unit = UNITS - 1 - step
        start_home(gs.at[unit + 1], grdb, 2, grd_recv, unit)
        grad = gs[unit + 1].astype(F32)
        fill_shifts(grad.reshape(PIX // COLS, COLS, C), shifts, True)
        parts = []
        for frame_off in range(3):
            taps = [
                wb[unit, frame_off * SLAB + tap * C : frame_off * SLAB + (tap + 1) * C]
                for tap in range(TAPS)
            ]
            parts.append(
                lax.dot_general(
                    shifts[...],
                    jnp.concatenate(taps, axis=1),
                    (((1,), (1,)), ((), ())),
                    preferred_element_type=F32,
                )
            )
        p0, p1, p2 = ([part[f * PLANE : (f + 1) * PLANE] for f in range(3)] for part in parts)
        gact = jnp.concatenate(
            [p0[0] + p0[1] + p0[2] + p1[0] + p1[1] + p2[0], p1[2] + p2[1], p2[2]], axis=0
        )
        xhat = xhat_s[unit]
        inner = gact.reshape(PIX // COLS, COLS, C) * slope_s[unit]
        mean_a = group_sum(jnp.sum(inner, axis=0)) * count
        mean_b = group_sum(jnp.sum(inner * xhat, axis=0)) * count
        slant = (inner - mean_a.reshape(1, 1, C) - xhat * mean_b.reshape(1, 1, C)) * rstd_s[unit].reshape(
            1, 1, C
        )
        gs[unit] = (grad + slant.reshape(PIX, C)).astype(BF16)
        start_home(gs.at[unit], grad_out, 3, ing_recv, unit)
        return 0

    lax.fori_loop(0, UNITS, backward, 0)

    @pl.when(half == 1)
    def _():
        hop_g.start()

    for slot in (1, 2):
        src, dst, recv = ((acts.at[y], actb, act_recv), (gs.at[y + 1], grdb, grd_recv))[slot - 1]
        finish_home(src, dst, slot, recv, y)
    arrived(actb, act_recv)
    arrived(grdb, grd_recv)

    def wgrad(clip, _):
        act = actb[clip].astype(F32)
        turned = [act[f * PLANE : (f + 1) * PLANE].T.astype(BF16) for f in range(FRAMES)]
        lhs = jnp.concatenate(
            [
                jnp.concatenate([turned[max(f - 2 + frame_off, 0)] for f in range(FRAMES)], axis=1)
                for frame_off in range(3)
            ],
            axis=0,
        )
        fill_shifts(grdb[clip].astype(F32).reshape(PIX // COLS, COLS, C), shifts, True)
        for tap in range(TAPS):
            block = dot(lhs, shifts[:, tap * C : (tap + 1) * C])
            for frame_off in range(3):
                at = (frame_off * TAPS + tap) * C
                part = block[frame_off * C : (frame_off + 1) * C]
                total[at : at + C] = total[at : at + C] + part
        return 0

    total[...] = jnp.zeros_like(total)
    lax.fori_loop(0, UNITS, wgrad, 0)

    chunk = WROWS // (4 * depth)
    for at_z in range(depth):
        for at_x in range(2):
            for at_core in range(2):
                start = (at_z * 4 + at_x * 2 + at_core) * chunk
                buf1[at_core, at_x, at_z] = total[start : start + chunk].astype(BF16)
    copy = remote(buf1.at[1 - core], got1, rs_send.at[0], rs_recv.at[0], dev(pipe, other_core))
    copy.start()
    copy.wait()
    buf2[...] = (buf1[core].astype(F32) + got1[...].astype(F32)).astype(BF16)
    copy = remote(buf2.at[1 - x_lo], got2, rs_send.at[1], rs_recv.at[1], dev(pipe, other_x))
    copy.start()
    copy.wait()
    buf3[...] = (buf2[x_lo].astype(F32) + got2[...].astype(F32)).astype(BF16)

    def z_copy(step):
        target = lax.rem(z + step, depth)
        return remote(
            buf3.at[target], got3.at[step - 1], z_send.at[step - 1], z_recv.at[step - 1], dev(pipe, z_peer(step))
        )

    for step in range(1, depth):
        z_copy(step).start()
    result = buf3[z].astype(F32)
    for step in range(1, depth):
        z_copy(step).wait_recv()
        result = result + got3[step - 1].astype(F32)
    wg_out[...] = result * scale

    for step in range(1, depth):
        z_copy(step).wait_send()
    for copy in sent:
        copy.wait_send()
    for slot, at in enumerate((yr, yo, yl)):
        gain_copy(at, slot).wait_send()
    for unit in range(UNITS):
        finish_home(xs.at[unit + 1], seg_out, 0, seg_recv, unit)
        finish_home(gs.at[unit], grad_out, 3, ing_recv, unit)

        @pl.when(unit != y)
        def _():
            to_home(acts.at[unit], actb, 1, act_recv, unit)[0].wait_send()
            to_home(gs.at[unit + 1], grdb, 2, grd_recv, unit)[0].wait_send()

    @pl.when(half == 0)
    def _():
        hop_x.wait_send()

    @pl.when(half == 1)
    def _():
        hop_g.wait_send()

    arrived(seg_out, seg_recv)
    arrived(grad_out, ing_recv)


def body(video, cotangent, weights, gains):
    micro = video.shape[0]
    devices = lax.axis_size("dp")
    depth = devices // 4
    chunk = WROWS // devices
    scale = 1.0 / math.sqrt(micro * devices * PIX)
    clip = (PIX, C)
    any_spec = pl.BlockSpec(memory_space=pl.ANY)
    dma = pltpu.SemaphoreType.DMA
    outputs, grads_out, share = pl.pallas_call(
        functools.partial(kernel, depth, scale),
        out_shape=(
            jax.ShapeDtypeStruct((micro, *clip), BF16),
            jax.ShapeDtypeStruct((micro, *clip), BF16),
            jax.ShapeDtypeStruct((chunk, C), F32),
        ),
        in_specs=[any_spec] * 4,
        out_specs=(any_spec, any_spec, pl.BlockSpec(memory_space=pltpu.VMEM)),
        scratch_shapes=[
            pltpu.VMEM((UNITS, WROWS, C), BF16),
            pltpu.VMEM((UNITS, 1, C), F32),
            pltpu.VMEM((UNITS + 1, *clip), BF16),
            pltpu.VMEM((UNITS + 1, *clip), BF16),
            pltpu.VMEM((UNITS, *clip), BF16),
            pltpu.VMEM((UNITS, PIX // COLS, COLS, C), F32),
            pltpu.VMEM((UNITS, PIX // COLS, COLS, C), F32),
            pltpu.VMEM((UNITS, 1, C), F32),
            pltpu.VMEM((PIX, SLAB), BF16),
            pltpu.VMEM((UNITS, *clip), BF16),
            pltpu.VMEM((UNITS, *clip), BF16),
            pltpu.VMEM((WROWS, C), F32),
            pltpu.VMEM((2, 2, depth, chunk, C), BF16),
            pltpu.VMEM((2, depth, chunk, C), BF16),
            pltpu.VMEM((2, depth, chunk, C), BF16),
            pltpu.VMEM((depth, chunk, C), BF16),
            pltpu.VMEM((depth, chunk, C), BF16),
            pltpu.VMEM((max(depth - 1, 1), chunk, C), BF16),
            dma((3,)),
            dma((12,)),
            dma((UNITS, 4)),
            dma((3,)),
            dma((UNITS,)),
            dma((2,)),
            dma((2,)),
            dma((4, UNITS)),
            dma((UNITS,)),
            dma((UNITS,)),
            dma((UNITS,)),
            dma((UNITS,)),
            dma((2,)),
            dma((2,)),
            dma((max(depth - 1, 1),)),
            dma((max(depth - 1, 1),)),
        ],
        compiler_params=pltpu.CompilerParams(collective_id=0, has_side_effects=True),
    )(
        video.reshape(micro, *clip),
        cotangent.reshape(micro, *clip),
        weights.reshape(WROWS, C),
        gains,
    )
    full = (1, micro, 1, FRAMES, ROWS, COLS, C)
    return (outputs.reshape(full), grads_out.reshape(full), share.reshape(1, -1))


def solution(mesh):
    in_specs = (
        P(None, "dp", None, None, None, None),
        P(None, "dp", None, None, None, None),
        P("pipe", None, None),
        P("pipe", None),
    )
    out_specs = (
        P("pipe", None, "dp", None, None, None, None),
        P("pipe", None, "dp", None, None, None, None),
        P("pipe", "dp"),
    )
    return jax.shard_map(body, mesh=mesh, in_specs=in_specs, out_specs=out_specs, check_vma=False)
```

time: 481 us -> 87.7 us (0.18)
  the two profiles are of different devices: /device:TPU:6 before, /device:TPU:1 now
where the time goes in v1:
time: 87.7 us; the launch traced here: 87.5 us
  Pallas kernels  82.8 us (94%)
  local copies, waits for them, and re-layouts  4.06 us (5%)
    pallas_call x1, Pallas kernels, body(): pl.pallas_call(functools.partial(kernel, depth, scale), out_shape=(jax.Sh...  82.8 us
    unnamed x5, local copies, waits for them, and re-layouts  4.06 us

profile of v1, /device:TPU:1, one launch (start us, length us, event | category | flops | bytes accessed | tf_op | source)
XLA Modules:
  0.0 87.5 jit_solution(17546414912827876598)
XLA Ops:
  0.6 82.8 %shard_map.67 = (bf16[4,384,128]{2,1,0:T(8,128)(2,1)}, bf16[4,384,128]{2,1,0:T(8,128)(2,1)}, f32[108,128]{1,0:T(8,128)}) custom-call(bf16[4,384,128]{2,1,0:T(8,128)(2,1)} %bitcast.17, bf16[4,384,128]{2,1,0:T(8,128)(2,1)} %bitcast.18, bf16[3456,128]{1,0:T(8,128)(2,1)} %bitcast.14, f32[1,128]{1,0:T(1,128)} %gains.1), custom_call_target="tpu_custom_call" | custom-call | tf_op jit(solution)/shard_map/pallas_call | solution.py:420
  83.5 1.5 %copy.11 = f32[1,1,108,128]{3,1,2,0:T(1,128)} copy(f32[1,1,108,128]{3,2,1,0:T(8,128)} %bitcast.19) | data formatting | bytes 110592
  85.0 0.0 copy-start
  85.0 1.8 %copy.14 = bf16[1,4,1,3,16,8,128]{6,5,4,3,2,1,0:T(8,128)(2,1)} copy(bf16[1,4,1,3,16,8,128]{6,5,4,3,2,1,0:T(8,128)(2,1)} %bitcast.16) | data formatting | bytes 786432
  86.8 0.0 copy-done
  86.8 0.7 copy.15
Async XLA Ops:
  85.0 1.8 %copy-start = (bf16[4,384,128]{2,1,0:T(8,128)(2,1)S(1)}, bf16[4,384,128]{2,1,0:T(8,128)(2,1)}, u32[]{:S(2)}) copy-start(bf16[4,384,128]{2,1,0:T(8,128)(2,1)} %get-tuple-element.7) | copy-start | bytes 1179652

commit v2 on v1

--- a/solution.py
+++ b/solution.py
@@ -16,7 +16,7 @@
 TAPS = 9
 SLAB = TAPS * C
 WROWS = 3 * SLAB
-QUARTER = WROWS // 4
+EIGHTH = WROWS // 8
 MESH = pl.DeviceIdType.MESH
 F32, BF16 = jnp.float32, jnp.bfloat16
 
@@ -115,6 +115,8 @@
     other_core = dp + 1 - 2 * core
     other_x = dp + 2 - 4 * x_lo
     other_half = pipe + UNITS - 2 * base
+    other_z = dp + 4 - 8 * lax.rem(z, 2)
+    owner = dp + half * (2 - 4 * x_lo)
 
     def dev(pipe_at, dp_at):
         return (pipe_at, dp_at)
@@ -132,17 +134,17 @@
     load_gain = pltpu.make_async_copy(gains, gbuf.at[y], load_sem.at[1])
     load_gain.start()
 
+    load_x = pltpu.make_async_copy(video.at[y], xs.at[0], load_sem.at[2])
+    cot_copy = remote(cot.at[y], gs.at[UNITS], hop_send.at[2], hop_recv.at[2], dev(pipe, other_x))
+
     @pl.when(half == 0)
     def _():
-        pltpu.make_async_copy(video.at[y], xs.at[0], load_sem.at[2]).start()
-
-    @pl.when(half == 1)
-    def _():
-        pltpu.make_async_copy(cot.at[y], gs.at[UNITS], load_sem.at[2]).start()
+        load_x.start()
 
     barrier = pltpu.get_barrier_semaphore()
     peers = [dev(base + at, dp) for at in (yr, yo, yl)]
-    peers += [dev(other_half, dp), dev(pipe, other_core), dev(pipe, other_x)]
+    peers += [dev(base + at, other_x) for at in (y, yr, yo, yl)]
+    peers += [dev(other_half, other_x), dev(pipe, other_core)]
     peers += [dev(pipe, z_peer(step)) for step in range(1, depth)]
     for peer in peers:
         pl.semaphore_signal(barrier, inc=1, device_id=peer, device_id_type=MESH)
@@ -154,96 +156,110 @@
     for slot, at in enumerate((yr, yo, yl)):
         gain_copy(at, slot).start()
 
-    qa = core * 2
-    qb = core * 2 + 1
+    @pl.when(half == 1)
+    def _():
+        cot_copy.start()
+
+    parity = lax.rem(x_lo + z, 2)
+    qa, qb = (parity * 2 + at for at in range(2))
+    pa, pb = ((1 - parity) * 2 + at for at in range(2))
     right, left, twin = dev(base + yr, dp), dev(base + yl, dp), dev(pipe, other_core)
-
-    def rows_of(quarter):
-        return pl.ds(pl.multiple_of(quarter * QUARTER, QUARTER), QUARTER)
+    near_x, near_z = dev(pipe, other_x), dev(pipe, other_z)
+
+    def rows_of(quarter, which):
+        return pl.ds(pl.multiple_of((quarter * 2 + which) * EIGHTH, EIGHTH), EIGHTH)
 
     def own(quarter, slot, target):
         return remote(
-            w.at[rows_of(quarter)],
-            wb.at[y, rows_of(quarter)],
+            w.at[rows_of(quarter, core)],
+            wb.at[y, rows_of(quarter, core)],
             w_send.at[slot],
-            w_recv.at[y, quarter],
+            w_recv.at[y, quarter * 2 + core],
             target,
         )
 
-    def relay(slab, quarter, slot, target):
-        piece = wb.at[slab, rows_of(quarter)]
-        return remote(piece, piece, w_send.at[slot], w_recv.at[slab, quarter], target)
-
-    first = [own(qa, 0, right), own(qb, 1, left), own(qb, 2, right), own(qa, 3, left)]
-    for copy in first:
+    def relay(slab, quarter, slot, target, which=core):
+        piece = wb.at[slab, rows_of(quarter, which)]
+        return remote(piece, piece, w_send.at[slot], w_recv.at[slab, quarter * 2 + which], target)
+
+    sent = [own(qa, 0, right), own(qb, 1, left), own(qb, 2, right), own(qa, 3, left)]
+    for copy in sent:
         copy.start()
     relays = [
-        (yl, qa, ((4, right), (6, twin))),
-        (yr, qb, ((5, left), (7, twin))),
-        (yl, qb, ((8, twin),)),
-        (yr, qa, ((9, twin),)),
-        (yo, qa, ((10, twin),)),
-        (yo, qb, ((11, twin),)),
+        (yl, qa, (right, twin, near_x)),
+        (yr, qb, (left, twin, near_z)),
+        (yl, qb, (twin, near_z)),
+        (yr, qa, (twin, near_x)),
+        (yl, pa, (twin,)),
+        (yr, pb, (twin,)),
+        (yo, qa, (twin, near_x)),
+        (yo, qb, (twin, near_z)),
+        (yr, pa, (twin,)),
+        (yl, pb, (twin,)),
+        (yo, pa, (twin,)),
+        (yo, pb, (twin,)),
     ]
-    sent = list(first)
     for slab, quarter, targets in relays:
         relay(slab, quarter, 0, right).wait_recv()
-        for slot, target in targets:
-            copy = relay(slab, quarter, slot, target)
+        for target in targets:
+            copy = relay(slab, quarter, len(sent), target)
             copy.start()
             sent.append(copy)
-    qc = (1 - core) * 2
     for slab in (yl, yr, yo):
-        for quarter in (qc, qc + 1):
-            relay(slab, quarter, 0, twin).wait_recv()
+        for quarter in range(4):
+            relay(slab, quarter, 0, twin, 1 - core).wait_recv()
     load_w.wait()
     load_gain.wait()
     for slot, at in enumerate((yr, yo, yl)):
         remote(gains, gbuf.at[at], gain_send.at[slot], gain_recv.at[at], dev(base + at, dp)).wait_recv()
 
-    def to_home(src, dst, slot, recv, unit):
-        away = remote(src, dst.at[y], out_send.at[slot, unit], recv.at[y], dev(base + unit, dp))
-        here = pltpu.make_async_copy(src, dst.at[y], out_send.at[slot, unit])
-        return away, here
+    def home(src, dst, slot, recv, unit, holder=dp):
+        local = (unit == y) & (holder == dp)
+
+        def away():
+            return remote(src, dst.at[y], out_send.at[slot, unit], recv.at[y], dev(base + unit, holder))
+
+        def here():
+            return pltpu.make_async_copy(src, dst.at[y], out_send.at[slot, unit])
+
+        return local, away, here
 
     def start_home(*args):
-        away, here = to_home(*args)
-        unit = args[-1]
-
-        @pl.when(unit != y)
+        local, away, here = home(*args)
+
+        @pl.when(jnp.logical_not(local))
         def _():
-            away.start()
-
-        @pl.when(unit == y)
+            away().start()
+
+        @pl.when(local)
         def _():
-            here.start()
+            here().start()
 
     def finish_home(*args):
-        away, here = to_home(*args)
-        unit = args[-1]
-
-        @pl.when(unit != y)
+        local, away, here = home(*args)
+
+        @pl.when(jnp.logical_not(local))
         def _():
-            away.wait_send()
-
-        @pl.when(unit == y)
+            away().wait_send()
+
+        @pl.when(local)
         def _():
-            here.wait()
-
-    def arrived(dst, recv):
-        for at in (yr, yo, yl):
-            remote(dst.at[at], dst.at[at], out_send.at[0, 0], recv.at[at], dev(base + at, dp)).wait_recv()
-
-    hop_x = remote(xs.at[UNITS], xs.at[0], hop_send.at[0], hop_recv.at[0], dev(other_half, dp))
-    hop_g = remote(gs.at[0], gs.at[UNITS], hop_send.at[1], hop_recv.at[1], dev(other_half, dp))
+            here().wait()
+
+    def arrived(dst, recv, places):
+        for at in places:
+            remote(dst.at[at], dst.at[at], out_send.at[0, 0], recv.at[at], near_x).wait_recv()
+
+    hop_x = remote(xs.at[UNITS], xs.at[0], hop_send.at[0], hop_recv.at[0], dev(other_half, other_x))
+    hop_g = remote(gs.at[0], gs.at[UNITS], hop_send.at[1], hop_recv.at[1], dev(other_half, other_x))
 
     @pl.when(half == 0)
     def _():
-        pltpu.make_async_copy(video.at[y], xs.at[0], load_sem.at[2]).wait()
+        load_x.wait()
 
     @pl.when(half == 1)
     def _():
-        pltpu.make_async_copy(cot.at[y], gs.at[UNITS], load_sem.at[2]).wait()
+        cot_copy.wait_recv()
         hop_x.wait_recv()
 
     count = 1.0 / (PIX * (C // GROUPS))
@@ -273,7 +289,7 @@
         for frame in range(FRAMES):
             at = slice(frame * PLANE, (frame + 1) * PLANE)
             xs[unit + 1, at] = (x[at] + branch[frame] + part2[at]).astype(BF16)
-        start_home(xs.at[unit + 1], seg_out, 0, seg_recv, unit)
+        start_home(xs.at[unit + 1], seg_out, 0, seg_recv, unit, owner)
         start_home(acts.at[unit], actb, 1, act_recv, unit)
         return 0
 
@@ -315,7 +331,7 @@
             1, 1, C
         )
         gs[unit] = (grad + slant.reshape(PIX, C)).astype(BF16)
-        start_home(gs.at[unit], grad_out, 3, ing_recv, unit)
+        start_home(gs.at[unit], grad_out, 3, ing_recv, unit, owner)
         return 0
 
     lax.fori_loop(0, UNITS, backward, 0)
@@ -324,11 +340,10 @@
     def _():
         hop_g.start()
 
-    for slot in (1, 2):
-        src, dst, recv = ((acts.at[y], actb, act_recv), (gs.at[y + 1], grdb, grd_recv))[slot - 1]
-        finish_home(src, dst, slot, recv, y)
-    arrived(actb, act_recv)
-    arrived(grdb, grd_recv)
+    home(acts.at[y], actb, 1, act_recv, y)[2]().wait()
+    home(gs.at[y + 1], grdb, 2, grd_recv, y)[2]().wait()
+    arrived(actb, act_recv, (yr, yo, yl))
+    arrived(grdb, grd_recv, (yr, yo, yl))
 
     def wgrad(clip, _):
         act = actb[clip].astype(F32)
@@ -388,13 +403,13 @@
     for slot, at in enumerate((yr, yo, yl)):
         gain_copy(at, slot).wait_send()
     for unit in range(UNITS):
-        finish_home(xs.at[unit + 1], seg_out, 0, seg_recv, unit)
-        finish_home(gs.at[unit], grad_out, 3, ing_recv, unit)
+        finish_home(xs.at[unit + 1], seg_out, 0, seg_recv, unit, owner)
+        finish_home(gs.at[unit], grad_out, 3, ing_recv, unit, owner)
 
         @pl.when(unit != y)
         def _():
-            to_home(acts.at[unit], actb, 1, act_recv, unit)[0].wait_send()
-            to_home(gs.at[unit + 1], grdb, 2, grd_recv, unit)[0].wait_send()
+            home(acts.at[unit], actb, 1, act_recv, unit)[1]().wait_send()
+            home(gs.at[unit + 1], grdb, 2, grd_recv, unit)[1]().wait_send()
 
     @pl.when(half == 0)
     def _():
@@ -402,10 +417,20 @@
 
     @pl.when(half == 1)
     def _():
+        cot_copy.wait_send()
         hop_g.wait_send()
-
-    arrived(seg_out, seg_recv)
-    arrived(grad_out, ing_recv)
+        arrived(seg_out, seg_recv, (y,))
+        arrived(grad_out, ing_recv, (y,))
+
+    arrived(seg_out, seg_recv, (yr, yo, yl))
+    arrived(grad_out, ing_recv, (yr, yo, yl))
+
+
+def write_results(seg, grad, share, seg_out, grad_out, share_out):
+    seg_out[...] = seg[...]
+    grad_out[...] = grad[...]
+    for row in range(share.shape[0]):
+        share_out[:, row * C : (row + 1) * C] = share[row : row + 1]
 
 
 def body(video, cotangent, weights, gains):
@@ -446,12 +471,12 @@
             pltpu.VMEM((depth, chunk, C), BF16),
             pltpu.VMEM((max(depth - 1, 1), chunk, C), BF16),
             dma((3,)),
-            dma((12,)),
-            dma((UNITS, 4)),
+            dma((24,)),
+            dma((UNITS, 8)),
             dma((3,)),
             dma((UNITS,)),
-            dma((2,)),
-            dma((2,)),
+            dma((3,)),
+            dma((3,)),
             dma((4, UNITS)),
             dma((UNITS,)),
             dma((UNITS,)),
@@ -469,8 +494,19 @@
         weights.reshape(WROWS, C),
         gains,
     )
+    whole = pl.BlockSpec(memory_space=pltpu.VMEM)
+    outputs, grads_out, share = pl.pallas_call(
+        write_results,
+        out_shape=(
+            jax.ShapeDtypeStruct((micro, *clip), BF16),
+            jax.ShapeDtypeStruct((micro, *clip), BF16),
+            jax.ShapeDtypeStruct((1, chunk * C), F32),
+        ),
+        in_specs=[whole] * 3,
+        out_specs=(whole,) * 3,
+    )(outputs, grads_out, share)
     full = (1, micro, 1, FRAMES, ROWS, COLS, C)
-    return (outputs.reshape(full), grads_out.reshape(full), share.reshape(1, -1))
+    return (outputs.reshape(full), grads_out.reshape(full), share)
 
 
 def solution(mesh):

time: 87.7 us -> 82.8 us (0.944); the launches traced: 87.5 us -> 81.7 us
  local copies, waits for them, and re-layouts: 4.06 us -> 0 us
  Pallas kernels: 82.8 us -> 81 us
    unnamed x5 -> x0, local copies, waits for them, and re-layouts: 4.06 us -> none
    pallas_call x1, Pallas kernels: 82.8 us -> 79 us  [body(): pl.pallas_call(functools.partial(kernel, depth, scale), out_shape=(jax.Sh...]
    pallas_call x0 -> x1, Pallas kernels: none -> 2.02 us  [body(): pl.pallas_call(write_results, out_shape=(jax.ShapeDtypeStruct((micro, *cl...]
where the time goes in v2:
time: 82.8 us; the launch traced here: 81.7 us
  Pallas kernels  81 us (98%)
    pallas_call x1, Pallas kernels, body(): pl.pallas_call(functools.partial(kernel, depth, scale), out_shape=(jax.Sh...  79 us
    pallas_call x1, Pallas kernels, body(): pl.pallas_call(write_results, out_shape=(jax.ShapeDtypeStruct((micro, *cl...  2.02 us

profile of v2, /device:TPU:1, one launch (start us, length us, event | category | flops | bytes accessed | tf_op | source)
XLA Modules:
  0.0 81.7 jit_solution(11535491166940863472)
XLA Ops:
  0.6 79.0 %shard_map.67 = (bf16[4,384,128]{2,1,0:T(8,128)(2,1)}, bf16[4,384,128]{2,1,0:T(8,128)(2,1)}, f32[108,128]{1,0:T(8,128)}) custom-call(bf16[4,384,128]{2,1,0:T(8,128)(2,1)} %bitcast.10, bf16[4,384,128]{2,1,0:T(8,128)(2,1)} %bitcast.11, bf16[3456,128]{1,0:T(8,128)(2,1)} %bitcast.9, f32[1,128]{1,0:T(1,128)} %gains.1), custom_call_target="tpu_custom_call" | custom-call | tf_op jit(solution)/shard_map/pallas_call | solution.py:445
  79.6 2.0 %shard_map.68 = (bf16[4,384,128]{2,1,0:T(8,128)(2,1)}, bf16[4,384,128]{2,1,0:T(8,128)(2,1)}, f32[1,13824]{1,0:T(1,128)}) custom-call(bf16[4,384,128]{2,1,0:T(8,128)(2,1)} %get-tuple-element.9.seg, bf16[4,384,128]{2,1,0:T(8,128)(2,1)} %get-tuple-element.10.grad, f32[108,128]{1,0:T(8,128)} %get-tuple-element.11.share), custom_call_target="tpu_custom_call" | custom-call | tf_op jit(solution)/shard_map/pallas_call | solution.py:498

commit v3 on v2

--- a/solution.py
+++ b/solution.py
@@ -28,7 +28,7 @@
     return jnp.sum(quad, axis=0, keepdims=True)
 
 
-def fill_shifts(field, dest, flip):
+def fill_shifts(field, dest, clip, flip):
     col = lax.broadcasted_iota(jnp.int32, field.shape, 1)
     for col_off in range(3):
         step = (1 - col_off) if flip else (col_off - 1)
@@ -48,8 +48,11 @@
                 rows = jnp.concatenate([planes[:, 1:], blank], axis=1)
             else:
                 rows = jnp.concatenate([blank, planes[:, : ROWS - 1]], axis=1)
-            at = (row_off * 3 + col_off) * C
-            dest[:, at : at + C] = rows.reshape(PIX, C).astype(BF16)
+            dest[row_off * 3 + col_off, clip] = rows.reshape(PIX, C).astype(BF16)
+
+
+def beside(parts):
+    return jnp.concatenate(parts, axis=1)
 
 
 def dot(lhs, rhs):
@@ -77,6 +80,7 @@
     shifts,
     actb,
     grdb,
+    turned,
     total,
     buf1,
     got1,
@@ -98,8 +102,6 @@
     ing_recv,
     rs_send,
     rs_recv,
-    z_send,
-    z_recv,
 ):
     pipe = lax.axis_index("pipe")
     dp = lax.axis_index("dp")
@@ -276,35 +278,55 @@
         sig = jax.nn.sigmoid(normed)
         act = normed * sig
         acts[unit] = act.reshape(PIX, C).astype(BF16)
-        fill_shifts(act, shifts, False)
+        fill_shifts(act, shifts, 0, False)
         xhat_s[unit] = xhat
         slope_s[unit] = (sig + act * (1.0 - sig)) * gain
         rstd_s[unit] = rstd
-        part0 = dot(shifts[:PLANE], wb[unit, :SLAB])
-        part1 = dot(shifts[: 2 * PLANE], wb[unit, SLAB : 2 * SLAB])
-        part2 = dot(shifts[...], wb[unit, 2 * SLAB :])
+        lhs = beside([shifts[tap, 0] for tap in range(TAPS)])
+        part0 = dot(lhs[:PLANE], wb[unit, :SLAB])
+        part1 = dot(lhs[: 2 * PLANE], wb[unit, SLAB : 2 * SLAB])
+        part2 = dot(lhs, wb[unit, 2 * SLAB :])
         x = x.reshape(PIX, C)
         early = part0 + part1[:PLANE]
         branch = (early, early, part0 + part1[PLANE:])
         for frame in range(FRAMES):
             at = slice(frame * PLANE, (frame + 1) * PLANE)
             xs[unit + 1, at] = (x[at] + branch[frame] + part2[at]).astype(BF16)
-        start_home(xs.at[unit + 1], seg_out, 0, seg_recv, unit, owner)
         start_home(acts.at[unit], actb, 1, act_recv, unit)
         return 0
 
     lax.fori_loop(0, UNITS, forward, 0)
 
+    def send_outputs():
+        for unit in range(UNITS):
+            start_home(xs.at[unit + 1], seg_out, 0, seg_recv, unit, owner)
+
+    def turn_acts():
+        home(acts.at[y], actb, 1, act_recv, y)[2]().wait()
+        arrived(actb, act_recv, (yr, yo, yl))
+
+        def turn(clip, _):
+            act = actb[clip].astype(F32)
+            frames = [act[f * PLANE : (f + 1) * PLANE].T.astype(BF16) for f in range(FRAMES)]
+            for frame_off in range(3):
+                turned[clip, frame_off] = beside([frames[max(f - 2 + frame_off, 0)] for f in range(FRAMES)])
+            return 0
+
+        lax.fori_loop(0, UNITS, turn, 0)
+
     @pl.when(half == 0)
     def _():
         hop_x.start()
+        send_outputs()
+        turn_acts()
         hop_g.wait_recv()
 
     def backward(step, _):
         unit = UNITS - 1 - step
         start_home(gs.at[unit + 1], grdb, 2, grd_recv, unit)
         grad = gs[unit + 1].astype(F32)
-        fill_shifts(grad.reshape(PIX // COLS, COLS, C), shifts, True)
+        fill_shifts(grad.reshape(PIX // COLS, COLS, C), shifts, 0, True)
+        lhs = beside([shifts[tap, 0] for tap in range(TAPS)])
         parts = []
         for frame_off in range(3):
             taps = [
@@ -313,8 +335,8 @@
             ]
             parts.append(
                 lax.dot_general(
-                    shifts[...],
-                    jnp.concatenate(taps, axis=1),
+                    lhs,
+                    beside(taps),
                     (((1,), (1,)), ((), ())),
                     preferred_element_type=F32,
                 )
@@ -331,73 +353,82 @@
             1, 1, C
         )
         gs[unit] = (grad + slant.reshape(PIX, C)).astype(BF16)
+        return 0
+
+    lax.fori_loop(0, UNITS, backward, 0)
+
+    @pl.when(half == 1)
+    def _():
+        hop_g.start()
+        turn_acts()
+
+    home(gs.at[y + 1], grdb, 2, grd_recv, y)[2]().wait()
+    arrived(grdb, grd_recv, (yr, yo, yl))
+
+    @pl.when(half == 1)
+    def _():
+        send_outputs()
+
+    for unit in range(UNITS):
         start_home(gs.at[unit], grad_out, 3, ing_recv, unit, owner)
+
+    def spread(clip, _):
+        fill_shifts(grdb[clip].astype(F32).reshape(PIX // COLS, COLS, C), shifts, clip, True)
         return 0
 
-    lax.fori_loop(0, UNITS, backward, 0)
-
-    @pl.when(half == 1)
-    def _():
-        hop_g.start()
-
-    home(acts.at[y], actb, 1, act_recv, y)[2]().wait()
-    home(gs.at[y + 1], grdb, 2, grd_recv, y)[2]().wait()
-    arrived(actb, act_recv, (yr, yo, yl))
-    arrived(grdb, grd_recv, (yr, yo, yl))
-
-    def wgrad(clip, _):
-        act = actb[clip].astype(F32)
-        turned = [act[f * PLANE : (f + 1) * PLANE].T.astype(BF16) for f in range(FRAMES)]
-        lhs = jnp.concatenate(
-            [
-                jnp.concatenate([turned[max(f - 2 + frame_off, 0)] for f in range(FRAMES)], axis=1)
-                for frame_off in range(3)
-            ],
-            axis=0,
-        )
-        fill_shifts(grdb[clip].astype(F32).reshape(PIX // COLS, COLS, C), shifts, True)
-        for tap in range(TAPS):
-            block = dot(lhs, shifts[:, tap * C : (tap + 1) * C])
+    lax.fori_loop(0, UNITS, spread, 0)
+    lhs = beside([turned[clip].reshape(3 * C, PIX) for clip in range(UNITS)])
+    for first in range(0, TAPS, 2):
+        taps = range(first, min(first + 2, TAPS))
+        block = dot(lhs, beside([shifts[tap].reshape(UNITS * PIX, C) for tap in taps]))
+        for tap in taps:
             for frame_off in range(3):
                 at = (frame_off * TAPS + tap) * C
-                part = block[frame_off * C : (frame_off + 1) * C]
-                total[at : at + C] = total[at : at + C] + part
-        return 0
-
-    total[...] = jnp.zeros_like(total)
-    lax.fori_loop(0, UNITS, wgrad, 0)
+                total[at : at + C] = block[frame_off * C : (frame_off + 1) * C, (tap - first) * C :][:, :C]
 
     chunk = WROWS // (4 * depth)
     for at_z in range(depth):
         for at_x in range(2):
             for at_core in range(2):
                 start = (at_z * 4 + at_x * 2 + at_core) * chunk
-                buf1[at_core, at_x, at_z] = total[start : start + chunk].astype(BF16)
-    copy = remote(buf1.at[1 - core], got1, rs_send.at[0], rs_recv.at[0], dev(pipe, other_core))
-    copy.start()
-    copy.wait()
-    buf2[...] = (buf1[core].astype(F32) + got1[...].astype(F32)).astype(BF16)
-    copy = remote(buf2.at[1 - x_lo], got2, rs_send.at[1], rs_recv.at[1], dev(pipe, other_x))
-    copy.start()
-    copy.wait()
-    buf3[...] = (buf2[x_lo].astype(F32) + got2[...].astype(F32)).astype(BF16)
-
-    def z_copy(step):
-        target = lax.rem(z + step, depth)
-        return remote(
-            buf3.at[target], got3.at[step - 1], z_send.at[step - 1], z_recv.at[step - 1], dev(pipe, z_peer(step))
-        )
-
-    for step in range(1, depth):
-        z_copy(step).start()
+                buf1[at_z, at_core, at_x] = total[start : start + chunk].astype(BF16)
+    steps = sorted(range(depth), key=lambda step: -min(step, depth - step))
+    places = [lax.rem(z + step, depth) for step in steps]
+
+    def core_copy(at):
+        return remote(buf1.at[at, 1 - core], got1.at[at], rs_send.at[0, at], rs_recv.at[0, at], twin)
+
+    def x_copy(at):
+        return remote(buf2.at[at, 1 - x_lo], got2.at[at], rs_send.at[1, at], rs_recv.at[1, at], near_x)
+
+    def z_copy(at):
+        target = dev(pipe, at * 4 + lax.rem(dp, 4))
+        return remote(buf3.at[at], got3.at[z], rs_send.at[2, at], rs_recv.at[2, z], target)
+
+    for at in places:
+        core_copy(at).start()
+    for at in places:
+        core_copy(at).wait_recv()
+        buf2[at] = (buf1[at, core].astype(F32) + got1[at].astype(F32)).astype(BF16)
+        x_copy(at).start()
+    for step, at in zip(steps, places):
+        x_copy(at).wait_recv()
+        buf3[at] = (buf2[at, x_lo].astype(F32) + got2[at].astype(F32)).astype(BF16)
+        if step:
+            z_copy(at).start()
     result = buf3[z].astype(F32)
-    for step in range(1, depth):
-        z_copy(step).wait_recv()
-        result = result + got3[step - 1].astype(F32)
+    for step in reversed(steps):
+        if step:
+            at = lax.rem(z + step, depth)
+            remote(got3.at[at], got3.at[at], rs_send.at[2, at], rs_recv.at[2, at], twin).wait_recv()
+            result = result + got3[at].astype(F32)
     wg_out[...] = result * scale
 
-    for step in range(1, depth):
-        z_copy(step).wait_send()
+    for step, at in zip(steps, places):
+        core_copy(at).wait_send()
+        x_copy(at).wait_send()
+        if step:
+            z_copy(at).wait_send()
     for copy in sent:
         copy.wait_send()
     for slot, at in enumerate((yr, yo, yl)):
@@ -426,11 +457,19 @@
     arrived(grad_out, ing_recv, (yr, yo, yl))
 
 
-def write_results(seg, grad, share, seg_out, grad_out, share_out):
-    seg_out[...] = seg[...]
-    grad_out[...] = grad[...]
+def write_results(seg, grad, share, seg_out, grad_out, share_out, flat, sem):
+    copies = [
+        pltpu.make_async_copy(seg, seg_out, sem.at[0]),
+        pltpu.make_async_copy(grad, grad_out, sem.at[1]),
+        pltpu.make_async_copy(flat, share_out, sem.at[2]),
+    ]
+    copies[0].start()
+    copies[1].start()
     for row in range(share.shape[0]):
-        share_out[:, row * C : (row + 1) * C] = share[row : row + 1]
+        flat[:, row * C : (row + 1) * C] = share[row : row + 1]
+    copies[2].start()
+    for copy in copies:
+        copy.wait()
 
 
 def body(video, cotangent, weights, gains):
@@ -449,7 +488,7 @@
             jax.ShapeDtypeStruct((micro, *clip), BF16),
             jax.ShapeDtypeStruct((chunk, C), F32),
         ),
-        in_specs=[any_spec] * 4,
+        in_specs=[pl.BlockSpec(memory_space=pltpu.HBM)] * 4,
         out_specs=(any_spec, any_spec, pl.BlockSpec(memory_space=pltpu.VMEM)),
         scratch_shapes=[
             pltpu.VMEM((UNITS, WROWS, C), BF16),
@@ -460,16 +499,17 @@
             pltpu.VMEM((UNITS, PIX // COLS, COLS, C), F32),
             pltpu.VMEM((UNITS, PIX // COLS, COLS, C), F32),
             pltpu.VMEM((UNITS, 1, C), F32),
-            pltpu.VMEM((PIX, SLAB), BF16),
+            pltpu.VMEM((TAPS, UNITS, *clip), BF16),
             pltpu.VMEM((UNITS, *clip), BF16),
             pltpu.VMEM((UNITS, *clip), BF16),
+            pltpu.VMEM((UNITS, 3, C, PIX), BF16),
             pltpu.VMEM((WROWS, C), F32),
-            pltpu.VMEM((2, 2, depth, chunk, C), BF16),
-            pltpu.VMEM((2, depth, chunk, C), BF16),
-            pltpu.VMEM((2, depth, chunk, C), BF16),
+            pltpu.VMEM((depth, 2, 2, chunk, C), BF16),
+            pltpu.VMEM((depth, 2, chunk, C), BF16),
+            pltpu.VMEM((depth, 2, chunk, C), BF16),
             pltpu.VMEM((depth, chunk, C), BF16),
             pltpu.VMEM((depth, chunk, C), BF16),
-            pltpu.VMEM((max(depth - 1, 1), chunk, C), BF16),
+            pltpu.VMEM((depth, chunk, C), BF16),
             dma((3,)),
             dma((24,)),
             dma((UNITS, 8)),
@@ -482,17 +522,20 @@
             dma((UNITS,)),
             dma((UNITS,)),
             dma((UNITS,)),
-            dma((2,)),
-            dma((2,)),
-            dma((max(depth - 1, 1),)),
-            dma((max(depth - 1, 1),)),
+            dma((3, depth)),
+            dma((3, depth)),
         ],
-        compiler_params=pltpu.CompilerParams(collective_id=0, has_side_effects=True),
+        compiler_params=pltpu.CompilerParams(collective_id=0, has_side_effects=True, vmem_limit_bytes=32 << 20),
     )(
-        video.reshape(micro, *clip),
-        cotangent.reshape(micro, *clip),
-        weights.reshape(WROWS, C),
-        gains,
+        *(
+            pltpu.with_memory_space_constraint(array, pltpu.HBM)
+            for array in (
+                video.reshape(micro, *clip),
+                cotangent.reshape(micro, *clip),
+                weights.reshape(WROWS, C),
+                gains,
+            )
+        )
     )
     whole = pl.BlockSpec(memory_space=pltpu.VMEM)
     outputs, grads_out, share = pl.pallas_call(
@@ -502,8 +545,10 @@
             jax.ShapeDtypeStruct((micro, *clip), BF16),
             jax.ShapeDtypeStruct((1, chunk * C), F32),
         ),
-        in_specs=[whole] * 3,
-        out_specs=(whole,) * 3,
+        in_specs=[any_spec, any_spec, whole],
+        out_specs=(pl.BlockSpec(memory_space=pltpu.HBM),) * 3,
+        scratch_shapes=[pltpu.VMEM((1, chunk * C), F32), dma((3,))],
+        compiler_params=pltpu.CompilerParams(vmem_limit_bytes=4 << 20),
     )(outputs, grads_out, share)
     full = (1, micro, 1, FRAMES, ROWS, COLS, C)
     return (outputs.reshape(full), grads_out.reshape(full), share)

time: 82.8 us -> 75.7 us (0.914)
  Pallas kernels: 81 us -> 73.8 us
    pallas_call x1, Pallas kernels: 79 us -> 72.9 us  [body(): pl.pallas_call(functools.partial(kernel, depth, scale), out_shape=(jax.Sh...]
    pallas_call x1, Pallas kernels: 2.02 us -> 0.91 us  [body(): pl.pallas_call(write_results, out_shape=(jax.ShapeDtypeStruct((micro, *cl...]
where the time goes in v3:
time: 75.7 us; the launch traced here: 74.5 us
  Pallas kernels  73.8 us (97%)
    pallas_call x1, Pallas kernels, body(): pl.pallas_call(functools.partial(kernel, depth, scale), out_shape=(jax.Sh...  72.9 us

profile of v3, /device:TPU:1, one launch (start us, length us, event | category | flops | bytes accessed | tf_op | source)
XLA Modules:
  0.0 74.5 jit_solution(17477712549300403598)
XLA Ops:
  0.6 72.9 %shard_map.67 = (bf16[4,384,128]{2,1,0:T(8,128)(2,1)S(1)}, bf16[4,384,128]{2,1,0:T(8,128)(2,1)S(1)}, f32[108,128]{1,0:T(8,128)S(1)}) custom-call(bf16[4,384,128]{2,1,0:T(8,128)(2,1)} %bitcast.10, bf16[4,384,128]{2,1,0:T(8,128)(2,1)} %bitcast.11, bf16[3456,128]{1,0:T(8,128)(2,1)} %bitcast.9, f32[1,128]{1,0:T(1,128)} %gains.1), custom_call_target="tpu_custom_call" | custom-call | tf_op jit(solution)/shard_map/pallas_call | solution.py:484
  73.5 0.9 %shard_map.68 = (bf16[4,384,128]{2,1,0:T(8,128)(2,1)}, bf16[4,384,128]{2,1,0:T(8,128)(2,1)}, f32[1,13824]{1,0:T(1,128)}) custom-call(bf16[4,384,128]{2,1,0:T(8,128)(2,1)S(1)} %get-tuple-element.9.seg, bf16[4,384,128]{2,1,0:T(8,128)(2,1)S(1)} %get-tuple-element.10.grad, f32[108,128]{1,0:T(8,128)S(1)} %get-tuple-element.11.share), custom_call_target="tpu_custom_call" | custom-call | tf_op jit(solution)/shard_map/pallas_call | solution.py:541

commit v4 on v3

--- a/solution.py
+++ b/solution.py
@@ -16,7 +16,8 @@
 TAPS = 9
 SLAB = TAPS * C
 WROWS = 3 * SLAB
-EIGHTH = WROWS // 8
+HALVES = 2
+PIECE = WROWS // (8 * HALVES)
 MESH = pl.DeviceIdType.MESH
 F32, BF16 = jnp.float32, jnp.bfloat16
 
@@ -73,6 +74,8 @@
     gbuf,
     xs,
     gs,
+    xs2,
+    gs2,
     acts,
     xhat_s,
     slope_s,
@@ -100,6 +103,8 @@
     act_recv,
     grd_recv,
     ing_recv,
+    swap_send,
+    swap_recv,
     rs_send,
     rs_recv,
 ):
@@ -118,7 +123,6 @@
     other_x = dp + 2 - 4 * x_lo
     other_half = pipe + UNITS - 2 * base
     other_z = dp + 4 - 8 * lax.rem(z, 2)
-    owner = dp + half * (2 - 4 * x_lo)
 
     def dev(pipe_at, dp_at):
         return (pipe_at, dp_at)
@@ -145,8 +149,7 @@
 
     barrier = pltpu.get_barrier_semaphore()
     peers = [dev(base + at, dp) for at in (yr, yo, yl)]
-    peers += [dev(base + at, other_x) for at in (y, yr, yo, yl)]
-    peers += [dev(other_half, other_x), dev(pipe, other_core)]
+    peers += [dev(pipe, other_x), dev(other_half, other_x), dev(pipe, other_core)]
     peers += [dev(pipe, z_peer(step)) for step in range(1, depth)]
     for peer in peers:
         pl.semaphore_signal(barrier, inc=1, device_id=peer, device_id_type=MESH)
@@ -168,58 +171,59 @@
     right, left, twin = dev(base + yr, dp), dev(base + yl, dp), dev(pipe, other_core)
     near_x, near_z = dev(pipe, other_x), dev(pipe, other_z)
 
-    def rows_of(quarter, which):
-        return pl.ds(pl.multiple_of((quarter * 2 + which) * EIGHTH, EIGHTH), EIGHTH)
-
-    def own(quarter, slot, target):
-        return remote(
-            w.at[rows_of(quarter, core)],
-            wb.at[y, rows_of(quarter, core)],
-            w_send.at[slot],
-            w_recv.at[y, quarter * 2 + core],
-            target,
-        )
-
-    def relay(slab, quarter, slot, target, which=core):
-        piece = wb.at[slab, rows_of(quarter, which)]
-        return remote(piece, piece, w_send.at[slot], w_recv.at[slab, quarter * 2 + which], target)
-
-    sent = [own(qa, 0, right), own(qb, 1, left), own(qb, 2, right), own(qa, 3, left)]
-    for copy in sent:
-        copy.start()
-    relays = [
-        (yl, qa, (right, twin, near_x)),
-        (yr, qb, (left, twin, near_z)),
-        (yl, qb, (twin, near_z)),
-        (yr, qa, (twin, near_x)),
-        (yl, pa, (twin,)),
-        (yr, pb, (twin,)),
-        (yo, qa, (twin, near_x)),
-        (yo, qb, (twin, near_z)),
-        (yr, pa, (twin,)),
-        (yl, pb, (twin,)),
-        (yo, pa, (twin,)),
-        (yo, pb, (twin,)),
+    def place_of(quarter, part, which):
+        return (quarter * 2 + which) * HALVES + part
+
+    def rows_of(place):
+        return pl.ds(pl.multiple_of(place * PIECE, PIECE), PIECE)
+
+    def own(quarter, part, slot, target):
+        place = place_of(quarter, part, core)
+        rows = rows_of(place)
+        return remote(w.at[rows], wb.at[y, rows], w_send.at[slot], w_recv.at[y, place], target)
+
+    def relay(slab, quarter, part, slot, target, which=core):
+        place = place_of(quarter, part, which)
+        piece = wb.at[slab, rows_of(place)]
+        return remote(piece, piece, w_send.at[slot], w_recv.at[slab, place], target)
+
+    sent = []
+    for quarters in ((qa, qb), (qb, qa)):
+        for part in range(HALVES):
+            for quarter, target in zip(quarters, (right, left)):
+                copy = own(quarter, part, len(sent), target)
+                copy.start()
+                sent.append(copy)
+    rounds = [
+        [(yl, qa, (right, near_x, twin)), (yr, qb, (left, near_z, twin))],
+        [(yl, qb, (near_z, twin)), (yr, qa, (near_x, twin))],
+        [(yl, pa, (twin,)), (yr, pb, (twin,))],
+        [(yo, qa, (near_x, twin)), (yo, qb, (near_z, twin))],
+        [(yr, pa, (twin,)), (yl, pb, (twin,))],
+        [(yo, pa, (twin,)), (yo, pb, (twin,))],
     ]
-    for slab, quarter, targets in relays:
-        relay(slab, quarter, 0, right).wait_recv()
-        for target in targets:
-            copy = relay(slab, quarter, len(sent), target)
-            copy.start()
-            sent.append(copy)
+    for group in rounds:
+        for part in range(HALVES):
+            for slab, quarter, targets in group:
+                relay(slab, quarter, part, 0, right).wait_recv()
+                for target in targets:
+                    copy = relay(slab, quarter, part, len(sent), target)
+                    copy.start()
+                    sent.append(copy)
     for slab in (yl, yr, yo):
         for quarter in range(4):
-            relay(slab, quarter, 0, twin, 1 - core).wait_recv()
+            for part in range(HALVES):
+                relay(slab, quarter, part, 0, twin, 1 - core).wait_recv()
     load_w.wait()
     load_gain.wait()
     for slot, at in enumerate((yr, yo, yl)):
         remote(gains, gbuf.at[at], gain_send.at[slot], gain_recv.at[at], dev(base + at, dp)).wait_recv()
 
-    def home(src, dst, slot, recv, unit, holder=dp):
-        local = (unit == y) & (holder == dp)
+    def home(src, dst, slot, recv, unit):
+        local = unit == y
 
         def away():
-            return remote(src, dst.at[y], out_send.at[slot, unit], recv.at[y], dev(base + unit, holder))
+            return remote(src, dst.at[y], out_send.at[slot, unit], recv.at[y], dev(base + unit, dp))
 
         def here():
             return pltpu.make_async_copy(src, dst.at[y], out_send.at[slot, unit])
@@ -251,6 +255,9 @@
     def arrived(dst, recv, places):
         for at in places:
             remote(dst.at[at], dst.at[at], out_send.at[0, 0], recv.at[at], near_x).wait_recv()
+
+    def swap(src, dst, slot, unit):
+        return remote(src.at[unit + 1 - slot], dst.at[unit], swap_send.at[slot, unit], swap_recv.at[slot, unit], near_x)
 
     hop_x = remote(xs.at[UNITS], xs.at[0], hop_send.at[0], hop_recv.at[0], dev(other_half, other_x))
     hop_g = remote(gs.at[0], gs.at[UNITS], hop_send.at[1], hop_recv.at[1], dev(other_half, other_x))
@@ -293,13 +300,26 @@
             at = slice(frame * PLANE, (frame + 1) * PLANE)
             xs[unit + 1, at] = (x[at] + branch[frame] + part2[at]).astype(BF16)
         start_home(acts.at[unit], actb, 1, act_recv, unit)
+
+        @pl.when(half == 1)
+        def _():
+            swap(xs, xs2, 0, unit).start()
+
         return 0
 
     lax.fori_loop(0, UNITS, forward, 0)
 
-    def send_outputs():
+    def send_outputs(kept, slot, swapped, dst, recv):
         for unit in range(UNITS):
-            start_home(xs.at[unit + 1], seg_out, 0, seg_recv, unit, owner)
+
+            @pl.when(half == 0)
+            def _():
+                start_home(kept.at[unit + 1 - slot // 3], dst, slot, recv, unit)
+
+            @pl.when(half == 1)
+            def _():
+                swap(kept, swapped, slot // 3, unit).wait_recv()
+                start_home(swapped.at[unit], dst, slot, recv, unit)
 
     def turn_acts():
         home(acts.at[y], actb, 1, act_recv, y)[2]().wait()
@@ -317,8 +337,11 @@
     @pl.when(half == 0)
     def _():
         hop_x.start()
-        send_outputs()
         turn_acts()
+
+    @pl.when(half == 0)
+    def _():
+        send_outputs(xs, 0, xs2, seg_out, seg_recv)
         hop_g.wait_recv()
 
     def backward(step, _):
@@ -353,6 +376,11 @@
             1, 1, C
         )
         gs[unit] = (grad + slant.reshape(PIX, C)).astype(BF16)
+
+        @pl.when(half == 1)
+        def _():
+            swap(gs, gs2, 1, unit).start()
+
         return 0
 
     lax.fori_loop(0, UNITS, backward, 0)
@@ -363,20 +391,23 @@
         turn_acts()
 
     home(gs.at[y + 1], grdb, 2, grd_recv, y)[2]().wait()
-    arrived(grdb, grd_recv, (yr, yo, yl))
-
-    @pl.when(half == 1)
-    def _():
-        send_outputs()
-
-    for unit in range(UNITS):
-        start_home(gs.at[unit], grad_out, 3, ing_recv, unit, owner)
-
-    def spread(clip, _):
+
+    def spread(step, _):
+        clip = lax.rem(y + step + (step // 2) * (5 - 2 * step), UNITS)
+
+        @pl.when(step > 0)
+        def _():
+            arrived(grdb, grd_recv, (clip,))
+
         fill_shifts(grdb[clip].astype(F32).reshape(PIX // COLS, COLS, C), shifts, clip, True)
         return 0
 
     lax.fori_loop(0, UNITS, spread, 0)
+
+    @pl.when(half == 1)
+    def _():
+        send_outputs(xs, 0, xs2, seg_out, seg_recv)
+
     lhs = beside([turned[clip].reshape(3 * C, PIX) for clip in range(UNITS)])
     for first in range(0, TAPS, 2):
         taps = range(first, min(first + 2, TAPS))
@@ -411,6 +442,7 @@
         core_copy(at).wait_recv()
         buf2[at] = (buf1[at, core].astype(F32) + got1[at].astype(F32)).astype(BF16)
         x_copy(at).start()
+    send_outputs(gs, 3, gs2, grad_out, ing_recv)
     for step, at in zip(steps, places):
         x_copy(at).wait_recv()
         buf3[at] = (buf2[at, x_lo].astype(F32) + got2[at].astype(F32)).astype(BF16)
@@ -434,8 +466,8 @@
     for slot, at in enumerate((yr, yo, yl)):
         gain_copy(at, slot).wait_send()
     for unit in range(UNITS):
-        finish_home(xs.at[unit + 1], seg_out, 0, seg_recv, unit, owner)
-        finish_home(gs.at[unit], grad_out, 3, ing_recv, unit, owner)
+        finish_home(xs2.at[unit], seg_out, 0, seg_recv, unit)
+        finish_home(gs2.at[unit], grad_out, 3, ing_recv, unit)
 
         @pl.when(unit != y)
         def _():
@@ -450,8 +482,9 @@
     def _():
         cot_copy.wait_send()
         hop_g.wait_send()
-        arrived(seg_out, seg_recv, (y,))
-        arrived(grad_out, ing_recv, (y,))
+        for unit in range(UNITS):
+            swap(xs, xs2, 0, unit).wait_send()
+            swap(gs, gs2, 1, unit).wait_send()
 
     arrived(seg_out, seg_recv, (yr, yo, yl))
     arrived(grad_out, ing_recv, (yr, yo, yl))
@@ -496,6 +529,8 @@
             pltpu.VMEM((UNITS + 1, *clip), BF16),
             pltpu.VMEM((UNITS + 1, *clip), BF16),
             pltpu.VMEM((UNITS, *clip), BF16),
+            pltpu.VMEM((UNITS, *clip), BF16),
+            pltpu.VMEM((UNITS, *clip), BF16),
             pltpu.VMEM((UNITS, PIX // COLS, COLS, C), F32),
             pltpu.VMEM((UNITS, PIX // COLS, COLS, C), F32),
             pltpu.VMEM((UNITS, 1, C), F32),
@@ -511,8 +546,8 @@
             pltpu.VMEM((depth, chunk, C), BF16),
             pltpu.VMEM((depth, chunk, C), BF16),
             dma((3,)),
-            dma((24,)),
-            dma((UNITS, 8)),
+            dma((24 * HALVES,)),
+            dma((UNITS, 8 * HALVES)),
             dma((3,)),
             dma((UNITS,)),
             dma((3,)),
@@ -522,6 +557,8 @@
             dma((UNITS,)),
             dma((UNITS,)),
             dma((UNITS,)),
+            dma((2, UNITS)),
+            dma((2, UNITS)),
             dma((3, depth)),
             dma((3, depth)),
         ],

time: 75.7 us -> 71.6 us (0.946); the launches traced: 74.5 us -> 71.5 us
  Pallas kernels: 73.8 us -> 70.9 us
    pallas_call x1, Pallas kernels: 72.9 us -> 70 us  [body(): pl.pallas_call(functools.partial(kernel, depth, scale), out_shape=(jax.Sh...]
where the time goes in v4:
time: 71.6 us; the launch traced here: 71.5 us
  Pallas kernels  70.9 us (99%)
    pallas_call x1, Pallas kernels, body(): pl.pallas_call(functools.partial(kernel, depth, scale), out_shape=(jax.Sh...  70 us

profile of v4, /device:TPU:1, one launch (start us, length us, event | category | flops | bytes accessed | tf_op | source)
XLA Modules:
  0.0 71.5 jit_solution(2756139509806693288)
XLA Ops:
  0.6 70.0 %shard_map.67 = (bf16[4,384,128]{2,1,0:T(8,128)(2,1)S(1)}, bf16[4,384,128]{2,1,0:T(8,128)(2,1)S(1)}, f32[108,128]{1,0:T(8,128)S(1)}) custom-call(bf16[4,384,128]{2,1,0:T(8,128)(2,1)} %bitcast.10, bf16[4,384,128]{2,1,0:T(8,128)(2,1)} %bitcast.11, bf16[3456,128]{1,0:T(8,128)(2,1)} %bitcast.9, f32[1,128]{1,0:T(1,128)} %gains.1), custom_call_target="tpu_custom_call" | custom-call | tf_op jit(solution)/shard_map/pallas_call | solution.py:517
  70.6 0.9 %shard_map.68 = (bf16[4,384,128]{2,1,0:T(8,128)(2,1)}, bf16[4,384,128]{2,1,0:T(8,128)(2,1)}, f32[1,13824]{1,0:T(1,128)}) custom-call(bf16[4,384,128]{2,1,0:T(8,128)(2,1)S(1)} %get-tuple-element.9.seg, bf16[4,384,128]{2,1,0:T(8,128)(2,1)S(1)} %get-tuple-element.10.grad, f32[108,128]{1,0:T(8,128)S(1)} %get-tuple-element.11.share), custom_call_target="tpu_custom_call" | custom-call | tf_op jit(solution)/shard_map/pallas_call | solution.py:578

commit v5 on v4

--- a/solution.py
+++ b/solution.py
@@ -39,17 +39,13 @@
             moved = jnp.where(col < COLS - 1, pltpu.roll(field, COLS - 1, 1), 0.0)
         else:
             moved = jnp.where(col > 0, pltpu.roll(field, 1, 1), 0.0)
-        planes = moved.reshape(FRAMES, ROWS, COLS, C)
-        blank = jnp.zeros((FRAMES, 1, COLS, C), F32)
-        for row_off in range(3):
-            step = (1 - row_off) if flip else (row_off - 1)
-            if step == 0:
-                rows = planes
-            elif step == 1:
-                rows = jnp.concatenate([planes[:, 1:], blank], axis=1)
-            else:
-                rows = jnp.concatenate([blank, planes[:, : ROWS - 1]], axis=1)
-            dest[row_off * 3 + col_off, clip] = rows.reshape(PIX, C).astype(BF16)
+        dest[col_off, clip, :, 1 : ROWS + 1] = moved.reshape(FRAMES, ROWS, COLS, C).astype(BF16)
+
+
+def shifted(kept, tap, flip, clips=1):
+    row_off, col_off = divmod(tap, 3)
+    first = 2 - row_off if flip else row_off
+    return kept[col_off, :clips, :, first : first + ROWS].reshape(clips * PIX, C)
 
 
 def beside(parts):
@@ -147,6 +143,9 @@
     def _():
         load_x.start()
 
+    for row in (0, ROWS + 1):
+        shifts[:, :, :, row] = jnp.zeros((3, UNITS, FRAMES, COLS, C), BF16)
+
     barrier = pltpu.get_barrier_semaphore()
     peers = [dev(base + at, dp) for at in (yr, yo, yl)]
     peers += [dev(pipe, other_x), dev(other_half, other_x), dev(pipe, other_core)]
@@ -289,10 +288,11 @@
         xhat_s[unit] = xhat
         slope_s[unit] = (sig + act * (1.0 - sig)) * gain
         rstd_s[unit] = rstd
-        lhs = beside([shifts[tap, 0] for tap in range(TAPS)])
+        lhs = beside([shifted(shifts, tap, False) for tap in range(TAPS)])
+        pair = dot(lhs[: 2 * PLANE], beside([wb[unit, SLAB : 2 * SLAB], wb[unit, 2 * SLAB :]]))
         part0 = dot(lhs[:PLANE], wb[unit, :SLAB])
-        part1 = dot(lhs[: 2 * PLANE], wb[unit, SLAB : 2 * SLAB])
-        part2 = dot(lhs, wb[unit, 2 * SLAB :])
+        part1 = pair[:, :C]
+        part2 = jnp.concatenate([pair[:, C:], dot(lhs[2 * PLANE :], wb[unit, 2 * SLAB :])], axis=0)
         x = x.reshape(PIX, C)
         early = part0 + part1[:PLANE]
         branch = (early, early, part0 + part1[PLANE:])
@@ -349,21 +349,16 @@
         start_home(gs.at[unit + 1], grdb, 2, grd_recv, unit)
         grad = gs[unit + 1].astype(F32)
         fill_shifts(grad.reshape(PIX // COLS, COLS, C), shifts, 0, True)
-        lhs = beside([shifts[tap, 0] for tap in range(TAPS)])
-        parts = []
-        for frame_off in range(3):
-            taps = [
-                wb[unit, frame_off * SLAB + tap * C : frame_off * SLAB + (tap + 1) * C]
-                for tap in range(TAPS)
-            ]
-            parts.append(
-                lax.dot_general(
-                    lhs,
-                    beside(taps),
-                    (((1,), (1,)), ((), ())),
-                    preferred_element_type=F32,
-                )
-            )
+        lhs = beside([shifted(shifts, tap, True) for tap in range(TAPS)])
+        flat = jnp.concatenate(
+            [
+                beside([wb[unit, k * SLAB + tap * C : k * SLAB + (tap + 1) * C] for tap in range(TAPS)])
+                for k in range(3)
+            ],
+            axis=0,
+        )
+        wide = lax.dot_general(lhs, flat, (((1,), (1,)), ((), ())), preferred_element_type=F32)
+        parts = [wide[:, k * C : (k + 1) * C] for k in range(3)]
         p0, p1, p2 = ([part[f * PLANE : (f + 1) * PLANE] for f in range(3)] for part in parts)
         gact = jnp.concatenate(
             [p0[0] + p0[1] + p0[2] + p1[0] + p1[1] + p2[0], p1[2] + p2[1], p2[2]], axis=0
@@ -411,7 +406,7 @@
     lhs = beside([turned[clip].reshape(3 * C, PIX) for clip in range(UNITS)])
     for first in range(0, TAPS, 2):
         taps = range(first, min(first + 2, TAPS))
-        block = dot(lhs, beside([shifts[tap].reshape(UNITS * PIX, C) for tap in taps]))
+        block = dot(lhs, beside([shifted(shifts, tap, True, UNITS) for tap in taps]))
         for tap in taps:
             for frame_off in range(3):
                 at = (frame_off * TAPS + tap) * C
@@ -534,7 +529,7 @@
             pltpu.VMEM((UNITS, PIX // COLS, COLS, C), F32),
             pltpu.VMEM((UNITS, PIX // COLS, COLS, C), F32),
             pltpu.VMEM((UNITS, 1, C), F32),
-            pltpu.VMEM((TAPS, UNITS, *clip), BF16),
+            pltpu.VMEM((3, UNITS, FRAMES, ROWS + 2, COLS, C), BF16),
             pltpu.VMEM((UNITS, *clip), BF16),
             pltpu.VMEM((UNITS, *clip), BF16),
             pltpu.VMEM((UNITS, 3, C, PIX), BF16),

time: 71.6 us -> 69 us (0.964)
  Pallas kernels: 70.9 us -> 68.3 us
    pallas_call x1, Pallas kernels: 70 us -> 67.4 us  [body(): pl.pallas_call(functools.partial(kernel, depth, scale), out_shape=(jax.Sh...]
where the time goes in v5:
time: 69 us
  Pallas kernels  68.3 us (99%)
    pallas_call x1, Pallas kernels, body(): pl.pallas_call(functools.partial(kernel, depth, scale), out_shape=(jax.Sh...  67.4 us

profile of v5, /device:TPU:1, one launch (start us, length us, event | category | flops | bytes accessed | tf_op | source)
XLA Modules:
  0.0 69.0 jit_solution(7616167326007614478)
XLA Ops:
  0.6 67.4 %shard_map.67 = (bf16[4,384,128]{2,1,0:T(8,128)(2,1)S(1)}, bf16[4,384,128]{2,1,0:T(8,128)(2,1)S(1)}, f32[108,128]{1,0:T(8,128)S(1)}) custom-call(bf16[4,384,128]{2,1,0:T(8,128)(2,1)} %bitcast.10, bf16[4,384,128]{2,1,0:T(8,128)(2,1)} %bitcast.11, bf16[3456,128]{1,0:T(8,128)(2,1)} %bitcast.9, f32[1,128]{1,0:T(1,128)} %gains.1), custom_call_target="tpu_custom_call" | custom-call | tf_op jit(solution)/shard_map/pallas_call | solution.py:512
  68.1 0.9 %shard_map.68 = (bf16[4,384,128]{2,1,0:T(8,128)(2,1)}, bf16[4,384,128]{2,1,0:T(8,128)(2,1)}, f32[1,13824]{1,0:T(1,128)}) custom-call(bf16[4,384,128]{2,1,0:T(8,128)(2,1)S(1)} %get-tuple-element.9.seg, bf16[4,384,128]{2,1,0:T(8,128)(2,1)S(1)} %get-tuple-element.10.grad, f32[108,128]{1,0:T(8,128)S(1)} %get-tuple-element.11.share), custom_call_target="tpu_custom_call" | custom-call | tf_op jit(solution)/shard_map/pallas_call | solution.py:573

commit v6 on v5

--- a/solution.py
+++ b/solution.py
@@ -76,6 +76,7 @@
     xhat_s,
     slope_s,
     rstd_s,
+    early_s,
     shifts,
     actb,
     grdb,
@@ -99,6 +100,7 @@
     act_recv,
     grd_recv,
     ing_recv,
+    known,
     swap_send,
     swap_recv,
     rs_send,
@@ -149,11 +151,128 @@
     barrier = pltpu.get_barrier_semaphore()
     peers = [dev(base + at, dp) for at in (yr, yo, yl)]
     peers += [dev(pipe, other_x), dev(other_half, other_x), dev(pipe, other_core)]
-    peers += [dev(pipe, z_peer(step)) for step in range(1, depth)]
+    peers += [dev(pipe, z_peer(step)) for step in (1, depth - 1)]
     for peer in peers:
         pl.semaphore_signal(barrier, inc=1, device_id=peer, device_id_type=MESH)
     pl.semaphore_wait(barrier, len(peers))
 
+    right, left, twin = dev(base + yr, dp), dev(base + yl, dp), dev(pipe, other_core)
+    near_x, near_z = dev(pipe, other_x), dev(pipe, other_z)
+
+    def home(src, dst, slot, recv, unit):
+        local = unit == y
+
+        def away():
+            return remote(src, dst.at[y], out_send.at[slot, unit], recv.at[y], dev(base + unit, dp))
+
+        def here():
+            return pltpu.make_async_copy(src, dst.at[y], out_send.at[slot, unit])
+
+        return local, away, here
+
+    def start_home(*args):
+        local, away, here = home(*args)
+
+        @pl.when(jnp.logical_not(local))
+        def _():
+            away().start()
+
+        @pl.when(local)
+        def _():
+            here().start()
+
+    def finish_home(*args):
+        local, away, here = home(*args)
+
+        @pl.when(jnp.logical_not(local))
+        def _():
+            away().wait_send()
+
+        @pl.when(local)
+        def _():
+            here().wait()
+
+    def arrived(dst, recv, places):
+        for at in places:
+            remote(dst.at[at], dst.at[at], out_send.at[0, 0], recv.at[at], near_x).wait_recv()
+
+    def swap(src, dst, slot, unit):
+        return remote(src.at[unit + 1 - slot], dst.at[unit], swap_send.at[slot, unit], swap_recv.at[slot, unit], near_x)
+
+    count = 1.0 / (PIX * (C // GROUPS))
+
+    def normalise(unit):
+        gain = gbuf[unit].reshape(1, 1, C)
+        x = xs[unit].astype(F32).reshape(PIX // COLS, COLS, C)
+        mean = group_sum(jnp.sum(x, axis=0)) * count
+        centred = x - mean.reshape(1, 1, C)
+        var = group_sum(jnp.sum(centred * centred, axis=0)) * count
+        rstd = lax.rsqrt(var + 1e-06)
+        xhat = centred * rstd.reshape(1, 1, C)
+        normed = xhat * gain
+        sig = jax.nn.sigmoid(normed)
+        act = normed * sig
+        acts[unit] = act.reshape(PIX, C).astype(BF16)
+        fill_shifts(act, shifts, 0, False)
+        xhat_s[unit] = xhat
+        slope_s[unit] = (sig + act * (1.0 - sig)) * gain
+        rstd_s[unit] = rstd
+
+    def convolve(unit, fresh=True):
+        if fresh:
+            start_home(acts.at[unit], actb, 1, act_recv, unit)
+        lhs = beside([shifted(shifts, tap, False) for tap in range(TAPS)])
+        pair = dot(lhs[: 2 * PLANE], beside([wb[unit, SLAB : 2 * SLAB], wb[unit, 2 * SLAB :]]))
+        part0 = dot(lhs[:PLANE], wb[unit, :SLAB])
+        part1 = pair[:, :C]
+        part2 = jnp.concatenate([pair[:, C:], dot(lhs[2 * PLANE :], wb[unit, 2 * SLAB :])], axis=0)
+        x = xs[unit].astype(F32)
+        early = part0 + part1[:PLANE]
+        branch = (early, early, part0 + part1[PLANE:])
+        for frame in range(FRAMES):
+            at = slice(frame * PLANE, (frame + 1) * PLANE)
+            xs[unit + 1, at] = (x[at] + branch[frame] + part2[at]).astype(BF16)
+
+        @pl.when(half == 1)
+        def _():
+            swap(xs, xs2, 0, unit).start()
+
+    def spread_back(unit):
+        grad = gs[unit + 1].astype(F32)
+        fill_shifts(grad.reshape(PIX // COLS, COLS, C), shifts, 0, True)
+        lhs = beside([shifted(shifts, tap, True) for tap in range(TAPS)])
+        flat = jnp.concatenate(
+            [
+                beside([wb[unit, k * SLAB + tap * C : k * SLAB + (tap + 1) * C] for tap in range(TAPS)])
+                for k in range(3)
+            ],
+            axis=0,
+        )
+        wide = lax.dot_general(lhs, flat, (((1,), (1,)), ((), ())), preferred_element_type=F32)
+        parts = [wide[:, k * C : (k + 1) * C] for k in range(3)]
+        p0, p1, p2 = ([part[f * PLANE : (f + 1) * PLANE] for f in range(3)] for part in parts)
+        return jnp.concatenate(
+            [p0[0] + p0[1] + p0[2] + p1[0] + p1[1] + p2[0], p1[2] + p2[1], p2[2]], axis=0
+        )
+
+    def through_norm(unit, gact):
+        xhat = xhat_s[unit]
+        inner = gact.reshape(PIX // COLS, COLS, C) * slope_s[unit]
+        mean_a = group_sum(jnp.sum(inner, axis=0)) * count
+        mean_b = group_sum(jnp.sum(inner * xhat, axis=0)) * count
+        slant = (inner - mean_a.reshape(1, 1, C) - xhat * mean_b.reshape(1, 1, C)) * rstd_s[unit].reshape(
+            1, 1, C
+        )
+        gs[unit] = (gs[unit + 1].astype(F32) + slant.reshape(PIX, C)).astype(BF16)
+
+        @pl.when(half == 1)
+        def _():
+            swap(gs, gs2, 1, unit).start()
+
+    def pass_on(step):
+        pl.semaphore_signal(known.at[step], inc=1, device_id=dev(pipe, z_peer(1)), device_id_type=MESH)
+        pl.semaphore_wait(known.at[step], 1)
+
     def gain_copy(at, slot):
         return remote(gains, gbuf.at[y], gain_send.at[slot], gain_recv.at[y], dev(base + at, dp))
 
@@ -167,8 +286,6 @@
     parity = lax.rem(x_lo + z, 2)
     qa, qb = (parity * 2 + at for at in range(2))
     pa, pb = ((1 - parity) * 2 + at for at in range(2))
-    right, left, twin = dev(base + yr, dp), dev(base + yl, dp), dev(pipe, other_core)
-    near_x, near_z = dev(pipe, other_x), dev(pipe, other_z)
 
     def place_of(quarter, part, which):
         return (quarter * 2 + which) * HALVES + part
@@ -193,6 +310,15 @@
                 copy = own(quarter, part, len(sent), target)
                 copy.start()
                 sent.append(copy)
+    load_gain.wait()
+    for slot, at in enumerate((yr, yo, yl)):
+        remote(gains, gbuf.at[at], gain_send.at[slot], gain_recv.at[at], dev(base + at, dp)).wait_recv()
+
+    @pl.when(half == 0)
+    def _():
+        load_x.wait()
+        normalise(0)
+
     rounds = [
         [(yl, qa, (right, near_x, twin)), (yr, qb, (left, near_z, twin))],
         [(yl, qb, (near_z, twin)), (yr, qa, (near_x, twin))],
@@ -214,100 +340,34 @@
             for part in range(HALVES):
                 relay(slab, quarter, part, 0, twin, 1 - core).wait_recv()
     load_w.wait()
-    load_gain.wait()
-    for slot, at in enumerate((yr, yo, yl)):
-        remote(gains, gbuf.at[at], gain_send.at[slot], gain_recv.at[at], dev(base + at, dp)).wait_recv()
-
-    def home(src, dst, slot, recv, unit):
-        local = unit == y
-
-        def away():
-            return remote(src, dst.at[y], out_send.at[slot, unit], recv.at[y], dev(base + unit, dp))
-
-        def here():
-            return pltpu.make_async_copy(src, dst.at[y], out_send.at[slot, unit])
-
-        return local, away, here
-
-    def start_home(*args):
-        local, away, here = home(*args)
-
-        @pl.when(jnp.logical_not(local))
-        def _():
-            away().start()
-
-        @pl.when(local)
-        def _():
-            here().start()
-
-    def finish_home(*args):
-        local, away, here = home(*args)
-
-        @pl.when(jnp.logical_not(local))
-        def _():
-            away().wait_send()
-
-        @pl.when(local)
-        def _():
-            here().wait()
-
-    def arrived(dst, recv, places):
-        for at in places:
-            remote(dst.at[at], dst.at[at], out_send.at[0, 0], recv.at[at], near_x).wait_recv()
-
-    def swap(src, dst, slot, unit):
-        return remote(src.at[unit + 1 - slot], dst.at[unit], swap_send.at[slot, unit], swap_recv.at[slot, unit], near_x)
 
     hop_x = remote(xs.at[UNITS], xs.at[0], hop_send.at[0], hop_recv.at[0], dev(other_half, other_x))
     hop_g = remote(gs.at[0], gs.at[UNITS], hop_send.at[1], hop_recv.at[1], dev(other_half, other_x))
 
+    @pl.when(half == 1)
+    def _():
+        cot_copy.wait_recv()
+        early_s[...] = spread_back(UNITS - 1)
+        for step in range(depth - 3):
+            pass_on(step)
+        hop_x.wait_recv()
+
+    def forward(unit, _):
+        normalise(unit)
+        convolve(unit)
+        return 0
+
     @pl.when(half == 0)
     def _():
-        load_x.wait()
+        convolve(0)
+
+    lax.fori_loop(1 - half, UNITS - half, forward, 0)
 
     @pl.when(half == 1)
     def _():
-        cot_copy.wait_recv()
-        hop_x.wait_recv()
-
-    count = 1.0 / (PIX * (C // GROUPS))
-
-    def forward(unit, _):
-        gain = gbuf[unit].reshape(1, 1, C)
-        x = xs[unit].astype(F32).reshape(PIX // COLS, COLS, C)
-        mean = group_sum(jnp.sum(x, axis=0)) * count
-        centred = x - mean.reshape(1, 1, C)
-        var = group_sum(jnp.sum(centred * centred, axis=0)) * count
-        rstd = lax.rsqrt(var + 1e-06)
-        xhat = centred * rstd.reshape(1, 1, C)
-        normed = xhat * gain
-        sig = jax.nn.sigmoid(normed)
-        act = normed * sig
-        acts[unit] = act.reshape(PIX, C).astype(BF16)
-        fill_shifts(act, shifts, 0, False)
-        xhat_s[unit] = xhat
-        slope_s[unit] = (sig + act * (1.0 - sig)) * gain
-        rstd_s[unit] = rstd
-        lhs = beside([shifted(shifts, tap, False) for tap in range(TAPS)])
-        pair = dot(lhs[: 2 * PLANE], beside([wb[unit, SLAB : 2 * SLAB], wb[unit, 2 * SLAB :]]))
-        part0 = dot(lhs[:PLANE], wb[unit, :SLAB])
-        part1 = pair[:, :C]
-        part2 = jnp.concatenate([pair[:, C:], dot(lhs[2 * PLANE :], wb[unit, 2 * SLAB :])], axis=0)
-        x = x.reshape(PIX, C)
-        early = part0 + part1[:PLANE]
-        branch = (early, early, part0 + part1[PLANE:])
-        for frame in range(FRAMES):
-            at = slice(frame * PLANE, (frame + 1) * PLANE)
-            xs[unit + 1, at] = (x[at] + branch[frame] + part2[at]).astype(BF16)
-        start_home(acts.at[unit], actb, 1, act_recv, unit)
-
-        @pl.when(half == 1)
-        def _():
-            swap(xs, xs2, 0, unit).start()
-
-        return 0
-
-    lax.fori_loop(0, UNITS, forward, 0)
+        normalise(UNITS - 1)
+        start_home(acts.at[UNITS - 1], actb, 1, act_recv, UNITS - 1)
+
 
     def send_outputs(kept, slot, swapped, dst, recv):
         for unit in range(UNITS):
@@ -342,47 +402,28 @@
     @pl.when(half == 0)
     def _():
         send_outputs(xs, 0, xs2, seg_out, seg_recv)
+        for step in range(depth - 3):
+            pass_on(step)
         hop_g.wait_recv()
 
     def backward(step, _):
         unit = UNITS - 1 - step
         start_home(gs.at[unit + 1], grdb, 2, grd_recv, unit)
-        grad = gs[unit + 1].astype(F32)
-        fill_shifts(grad.reshape(PIX // COLS, COLS, C), shifts, 0, True)
-        lhs = beside([shifted(shifts, tap, True) for tap in range(TAPS)])
-        flat = jnp.concatenate(
-            [
-                beside([wb[unit, k * SLAB + tap * C : k * SLAB + (tap + 1) * C] for tap in range(TAPS)])
-                for k in range(3)
-            ],
-            axis=0,
-        )
-        wide = lax.dot_general(lhs, flat, (((1,), (1,)), ((), ())), preferred_element_type=F32)
-        parts = [wide[:, k * C : (k + 1) * C] for k in range(3)]
-        p0, p1, p2 = ([part[f * PLANE : (f + 1) * PLANE] for f in range(3)] for part in parts)
-        gact = jnp.concatenate(
-            [p0[0] + p0[1] + p0[2] + p1[0] + p1[1] + p2[0], p1[2] + p2[1], p2[2]], axis=0
-        )
-        xhat = xhat_s[unit]
-        inner = gact.reshape(PIX // COLS, COLS, C) * slope_s[unit]
-        mean_a = group_sum(jnp.sum(inner, axis=0)) * count
-        mean_b = group_sum(jnp.sum(inner * xhat, axis=0)) * count
-        slant = (inner - mean_a.reshape(1, 1, C) - xhat * mean_b.reshape(1, 1, C)) * rstd_s[unit].reshape(
-            1, 1, C
-        )
-        gs[unit] = (grad + slant.reshape(PIX, C)).astype(BF16)
-
-        @pl.when(half == 1)
-        def _():
-            swap(gs, gs2, 1, unit).start()
-
+        through_norm(unit, spread_back(unit))
         return 0
 
-    lax.fori_loop(0, UNITS, backward, 0)
-
     @pl.when(half == 1)
     def _():
+        start_home(gs.at[UNITS], grdb, 2, grd_recv, UNITS - 1)
+        through_norm(UNITS - 1, early_s[...])
+
+    lax.fori_loop(half, UNITS, backward, 0)
+
+    @pl.when(half == 1)
+    def _():
         hop_g.start()
+        fill_shifts(acts[UNITS - 1].astype(F32).reshape(PIX // COLS, COLS, C), shifts, 0, False)
+        convolve(UNITS - 1, False)
         turn_acts()
 
     home(gs.at[y + 1], grdb, 2, grd_recv, y)[2]().wait()
@@ -529,6 +570,7 @@
             pltpu.VMEM((UNITS, PIX // COLS, COLS, C), F32),
             pltpu.VMEM((UNITS, PIX // COLS, COLS, C), F32),
             pltpu.VMEM((UNITS, 1, C), F32),
+            pltpu.VMEM(clip, F32),
             pltpu.VMEM((3, UNITS, FRAMES, ROWS + 2, COLS, C), BF16),
             pltpu.VMEM((UNITS, *clip), BF16),
             pltpu.VMEM((UNITS, *clip), BF16),
@@ -552,6 +594,7 @@
             dma((UNITS,)),
             dma((UNITS,)),
             dma((UNITS,)),
+            pltpu.SemaphoreType.REGULAR((depth - 3,)),
             dma((2, UNITS)),
             dma((2, UNITS)),
             dma((3, depth)),

time: 69 us -> 67.8 us (0.983)
  Pallas kernels: 68.3 us -> 67.1 us
    pallas_call x1, Pallas kernels: 67.4 us -> 66.2 us  [body(): pl.pallas_call(functools.partial(kernel, depth, scale), out_shape=(jax.Sh...]
where the time goes in v6:
time: 67.8 us
  Pallas kernels  67.1 us (99%)
    pallas_call x1, Pallas kernels, body(): pl.pallas_call(functools.partial(kernel, depth, scale), out_shape=(jax.Sh...  66.2 us

profile of v6, /device:TPU:1, one launch (start us, length us, event | category | flops | bytes accessed | tf_op | source)
XLA Modules:
  0.0 67.8 jit_solution(12699463646094682060)
XLA Ops:
  0.6 66.2 %shard_map.67 = (bf16[4,384,128]{2,1,0:T(8,128)(2,1)S(1)}, bf16[4,384,128]{2,1,0:T(8,128)(2,1)S(1)}, f32[108,128]{1,0:T(8,128)S(1)}) custom-call(bf16[4,384,128]{2,1,0:T(8,128)(2,1)} %bitcast.10, bf16[4,384,128]{2,1,0:T(8,128)(2,1)} %bitcast.11, bf16[3456,128]{1,0:T(8,128)(2,1)} %bitcast.9, f32[1,128]{1,0:T(1,128)} %gains.1), custom_call_target="tpu_custom_call" | custom-call | tf_op jit(solution)/shard_map/pallas_call | solution.py:553
  66.8 0.9 %shard_map.68 = (bf16[4,384,128]{2,1,0:T(8,128)(2,1)}, bf16[4,384,128]{2,1,0:T(8,128)(2,1)}, f32[1,13824]{1,0:T(1,128)}) custom-call(bf16[4,384,128]{2,1,0:T(8,128)(2,1)S(1)} %get-tuple-element.9.seg, bf16[4,384,128]{2,1,0:T(8,128)(2,1)S(1)} %get-tuple-element.10.grad, f32[108,128]{1,0:T(8,128)S(1)} %get-tuple-element.11.share), custom_call_target="tpu_custom_call" | custom-call | tf_op jit(solution)/shard_map/pallas_call | solution.py:616

commit v7 on v6

--- a/solution.py
+++ b/solution.py
@@ -440,10 +440,6 @@
 
     lax.fori_loop(0, UNITS, spread, 0)
 
-    @pl.when(half == 1)
-    def _():
-        send_outputs(xs, 0, xs2, seg_out, seg_recv)
-
     lhs = beside([turned[clip].reshape(3 * C, PIX) for clip in range(UNITS)])
     for first in range(0, TAPS, 2):
         taps = range(first, min(first + 2, TAPS))
@@ -454,16 +450,18 @@
                 total[at : at + C] = block[frame_off * C : (frame_off + 1) * C, (tap - first) * C :][:, :C]
 
     chunk = WROWS // (4 * depth)
+
+    def core_copy(at):
+        return remote(buf1.at[at, 1 - core], got1.at[at], rs_send.at[0, at], rs_recv.at[0, at], twin)
+
     for at_z in range(depth):
         for at_x in range(2):
             for at_core in range(2):
                 start = (at_z * 4 + at_x * 2 + at_core) * chunk
                 buf1[at_z, at_core, at_x] = total[start : start + chunk].astype(BF16)
+        core_copy(at_z).start()
     steps = sorted(range(depth), key=lambda step: -min(step, depth - step))
     places = [lax.rem(z + step, depth) for step in steps]
-
-    def core_copy(at):
-        return remote(buf1.at[at, 1 - core], got1.at[at], rs_send.at[0, at], rs_recv.at[0, at], twin)
 
     def x_copy(at):
         return remote(buf2.at[at, 1 - x_lo], got2.at[at], rs_send.at[1, at], rs_recv.at[1, at], near_x)
@@ -472,12 +470,15 @@
         target = dev(pipe, at * 4 + lax.rem(dp, 4))
         return remote(buf3.at[at], got3.at[z], rs_send.at[2, at], rs_recv.at[2, z], target)
 
-    for at in places:
-        core_copy(at).start()
     for at in places:
         core_copy(at).wait_recv()
         buf2[at] = (buf1[at, core].astype(F32) + got1[at].astype(F32)).astype(BF16)
         x_copy(at).start()
+
+    @pl.when(half == 1)
+    def _():
+        send_outputs(xs, 0, xs2, seg_out, seg_recv)
+
     send_outputs(gs, 3, gs2, grad_out, ing_recv)
     for step, at in zip(steps, places):
         x_copy(at).wait_recv()

time: 67.8 us -> 67.9 us (level)
  no operation moved by 1% of the time
where the time goes in v7:
time: 67.9 us; the launch traced here: 67.8 us
  Pallas kernels  67.2 us (99%)
    pallas_call x1, Pallas kernels, body(): pl.pallas_call(functools.partial(kernel, depth, scale), out_shape=(jax.Sh...  66.3 us

profile of v7, /device:TPU:1, one launch (start us, length us, event | category | flops | bytes accessed | tf_op | source)
XLA Modules:
  0.0 67.8 jit_solution(10367975591914583825)
XLA Ops:
  0.6 66.3 %shard_map.67 = (bf16[4,384,128]{2,1,0:T(8,128)(2,1)S(1)}, bf16[4,384,128]{2,1,0:T(8,128)(2,1)S(1)}, f32[108,128]{1,0:T(8,128)S(1)}) custom-call(bf16[4,384,128]{2,1,0:T(8,128)(2,1)} %bitcast.10, bf16[4,384,128]{2,1,0:T(8,128)(2,1)} %bitcast.11, bf16[3456,128]{1,0:T(8,128)(2,1)} %bitcast.9, f32[1,128]{1,0:T(1,128)} %gains.1), custom_call_target="tpu_custom_call" | custom-call | tf_op jit(solution)/shard_map/pallas_call | solution.py:554
  66.9 0.9 %shard_map.68 = (bf16[4,384,128]{2,1,0:T(8,128)(2,1)}, bf16[4,384,128]{2,1,0:T(8,128)(2,1)}, f32[1,13824]{1,0:T(1,128)}) custom-call(bf16[4,384,128]{2,1,0:T(8,128)(2,1)S(1)} %get-tuple-element.9.seg, bf16[4,384,128]{2,1,0:T(8,128)(2,1)S(1)} %get-tuple-element.10.grad, f32[108,128]{1,0:T(8,128)S(1)} %get-tuple-element.11.share), custom_call_target="tpu_custom_call" | custom-call | tf_op jit(solution)/shard_map/pallas_call | solution.py:617

commit v8 on v7

--- a/solution.py
+++ b/solution.py
@@ -154,6 +154,8 @@
     peers += [dev(pipe, z_peer(step)) for step in (1, depth - 1)]
     for peer in peers:
         pl.semaphore_signal(barrier, inc=1, device_id=peer, device_id_type=MESH)
+    load_w.wait()
+    load_gain.wait()
     pl.semaphore_wait(barrier, len(peers))
 
     right, left, twin = dev(base + yr, dp), dev(base + yl, dp), dev(pipe, other_core)
@@ -274,7 +276,7 @@
         pl.semaphore_wait(known.at[step], 1)
 
     def gain_copy(at, slot):
-        return remote(gains, gbuf.at[y], gain_send.at[slot], gain_recv.at[y], dev(base + at, dp))
+        return remote(gbuf.at[y], gbuf.at[y], gain_send.at[slot], gain_recv.at[y], dev(base + at, dp))
 
     for slot, at in enumerate((yr, yo, yl)):
         gain_copy(at, slot).start()
@@ -296,7 +298,7 @@
     def own(quarter, part, slot, target):
         place = place_of(quarter, part, core)
         rows = rows_of(place)
-        return remote(w.at[rows], wb.at[y, rows], w_send.at[slot], w_recv.at[y, place], target)
+        return remote(wb.at[y, rows], wb.at[y, rows], w_send.at[slot], w_recv.at[y, place], target)
 
     def relay(slab, quarter, part, slot, target, which=core):
         place = place_of(quarter, part, which)
@@ -310,7 +312,6 @@
                 copy = own(quarter, part, len(sent), target)
                 copy.start()
                 sent.append(copy)
-    load_gain.wait()
     for slot, at in enumerate((yr, yo, yl)):
         remote(gains, gbuf.at[at], gain_send.at[slot], gain_recv.at[at], dev(base + at, dp)).wait_recv()
 
@@ -339,7 +340,6 @@
         for quarter in range(4):
             for part in range(HALVES):
                 relay(slab, quarter, part, 0, twin, 1 - core).wait_recv()
-    load_w.wait()
 
     hop_x = remote(xs.at[UNITS], xs.at[0], hop_send.at[0], hop_recv.at[0], dev(other_half, other_x))
     hop_g = remote(gs.at[0], gs.at[UNITS], hop_send.at[1], hop_recv.at[1], dev(other_half, other_x))

time: 67.9 us -> 67.8 us (level)
  no operation moved by 1% of the time
where the time goes in v8:
time: 67.8 us; the launch traced here: 67.6 us
  Pallas kernels  67 us (99%)
    pallas_call x1, Pallas kernels, body(): pl.pallas_call(functools.partial(kernel, depth, scale), out_shape=(jax.Sh...  66.1 us

profile of v8, /device:TPU:1, one launch (start us, length us, event | category | flops | bytes accessed | tf_op | source)
XLA Modules:
  0.0 67.6 jit_solution(6938872374017688872)
XLA Ops:
  0.6 66.1 %shard_map.67 = (bf16[4,384,128]{2,1,0:T(8,128)(2,1)S(1)}, bf16[4,384,128]{2,1,0:T(8,128)(2,1)S(1)}, f32[108,128]{1,0:T(8,128)S(1)}) custom-call(bf16[4,384,128]{2,1,0:T(8,128)(2,1)} %bitcast.10, bf16[4,384,128]{2,1,0:T(8,128)(2,1)} %bitcast.11, bf16[3456,128]{1,0:T(8,128)(2,1)} %bitcast.9, f32[1,128]{1,0:T(1,128)} %gains.1), custom_call_target="tpu_custom_call" | custom-call | tf_op jit(solution)/shard_map/pallas_call | solution.py:554
  66.7 0.9 %shard_map.68 = (bf16[4,384,128]{2,1,0:T(8,128)(2,1)}, bf16[4,384,128]{2,1,0:T(8,128)(2,1)}, f32[1,13824]{1,0:T(1,128)}) custom-call(bf16[4,384,128]{2,1,0:T(8,128)(2,1)S(1)} %get-tuple-element.9.seg, bf16[4,384,128]{2,1,0:T(8,128)(2,1)S(1)} %get-tuple-element.10.grad, f32[108,128]{1,0:T(8,128)S(1)} %get-tuple-element.11.share), custom_call_target="tpu_custom_call" | custom-call | tf_op jit(solution)/shard_map/pallas_call | solution.py:617

commit v9 on v8

--- a/solution.py
+++ b/solution.py
@@ -312,12 +312,18 @@
                 copy = own(quarter, part, len(sent), target)
                 copy.start()
                 sent.append(copy)
-    for slot, at in enumerate((yr, yo, yl)):
-        remote(gains, gbuf.at[at], gain_send.at[slot], gain_recv.at[at], dev(base + at, dp)).wait_recv()
+    def gain_arrived(at):
+        remote(gbuf.at[at], gbuf.at[at], gain_send.at[0], gain_recv.at[at], twin).wait_recv()
+
 
     @pl.when(half == 0)
     def _():
         load_x.wait()
+
+        @pl.when(y != 0)
+        def _():
+            gain_arrived(0)
+
         normalise(0)
 
     rounds = [
@@ -336,6 +342,12 @@
                     copy = relay(slab, quarter, part, len(sent), target)
                     copy.start()
                     sent.append(copy)
+    for at in (yr, yo, yl):
+
+        @pl.when((at != 0) | (half == 1))
+        def _():
+            gain_arrived(at)
+
     for slab in (yl, yr, yo):
         for quarter in range(4):
             for part in range(HALVES):

time: 67.8 us -> 67.7 us (level)
  no operation moved by 1% of the time
where the time goes in v9:
time: 67.7 us; the launch traced here: 67.6 us
  Pallas kernels  67 us (99%)
    pallas_call x1, Pallas kernels, body(): pl.pallas_call(functools.partial(kernel, depth, scale), out_shape=(jax.Sh...  66 us

profile of v9, /device:TPU:1, one launch (start us, length us, event | category | flops | bytes accessed | tf_op | source)
XLA Modules:
  0.0 67.6 jit_solution(10724365948179249691)
XLA Ops:
  0.6 66.0 %shard_map.67 = (bf16[4,384,128]{2,1,0:T(8,128)(2,1)S(1)}, bf16[4,384,128]{2,1,0:T(8,128)(2,1)S(1)}, f32[108,128]{1,0:T(8,128)S(1)}) custom-call(bf16[4,384,128]{2,1,0:T(8,128)(2,1)} %bitcast.10, bf16[4,384,128]{2,1,0:T(8,128)(2,1)} %bitcast.11, bf16[3456,128]{1,0:T(8,128)(2,1)} %bitcast.9, f32[1,128]{1,0:T(1,128)} %gains.1), custom_call_target="tpu_custom_call" | custom-call | tf_op jit(solution)/shard_map/pallas_call | solution.py:566
  66.7 0.9 %shard_map.68 = (bf16[4,384,128]{2,1,0:T(8,128)(2,1)}, bf16[4,384,128]{2,1,0:T(8,128)(2,1)}, f32[1,13824]{1,0:T(1,128)}) custom-call(bf16[4,384,128]{2,1,0:T(8,128)(2,1)S(1)} %get-tuple-element.9.seg, bf16[4,384,128]{2,1,0:T(8,128)(2,1)S(1)} %get-tuple-element.10.grad, f32[108,128]{1,0:T(8,128)S(1)} %get-tuple-element.11.share), custom_call_target="tpu_custom_call" | custom-call | tf_op jit(solution)/shard_map/pallas_call | solution.py:629
